TPU v7x, 32 devices: a whole 2x2x4 slice. The times are simulated.
32 devices in a mesh: layer: 4 (over x, core), feat: 4 (over z), par: 2 (over y).
Axes of the slice: x: 2, y: 2, z: 4, core: 2. Of those that a mesh axis runs over, the one named last changes fastest.
Arguments:
- residual: bfloat16 [4, 512, 2304], P('layer'), may hold values from -6 to 6
- norm_gain: float32 [4, 2304], P('layer'), may hold values from 0.5 to 1.5
- gate_weight: bfloat16 [4, 2304, 9216], P('layer', None, ('feat', 'par')), may hold values from -0.125 to 0.125
- up_weight: bfloat16 [4, 2304, 9216], P('layer', None, ('feat', 'par')), may hold values from -0.125 to 0.125
- down_weight: bfloat16 [4, 9216, 2304], P('layer', ('feat', 'par')), may hold values from -0.0625 to 0.0625
- enc_weight: float32 [4, 2304, 8192], P('layer', 'par', 'feat'), may hold values from -0.125 to 0.125
- enc_bias: float32 [4, 8192], P('layer', 'feat'), may hold values from -1 to 0.5
- dec_weight: bfloat16 [4, 2, 2, 8192, 2304], P('layer', 'par', None, 'feat'), may hold values from -0.0625 to 0.0625
- dec_bias: float32 [4, 2304], replicated, may hold values from -3 to 3
Outputs:
- enc_grad: float32 [4, 2304, 8192], P('layer', 'par', 'feat')
- enc_bias_grad: float32 [4, 8192], P('layer', 'feat')
- dec_grad: bfloat16 [4, 2, 2, 8192, 2304], P('layer', 'par', None, 'feat')
All inputs are finite; a program needn't handle non-finite values.
Results may differ from a plain program's by a relative error of at most 0.007.
Values may be sent and summed in bfloat16 or wider, within the bound.
No kernel may reach another device: no remote copies, remote signals or barrier semaphores. Data moves between devices by JAX's collectives and lax.ppermute only.
A program may use at most 192 MiB of HBM per device.

v0:
```python
import jax
import jax.numpy as jnp
from jax import lax
from jax.sharding import PartitionSpec as P


def partner_2(value, axis, stride):
    mask = 2**stride
    pairs = [(source, source ^ mask) for source in range(lax.axis_size(axis))]
    return lax.ppermute(value, axis, pairs)


def rms_normed(rows_in, gain_row):
    values = rows_in.astype(jnp.float32)
    scaling = lax.rsqrt(jnp.mean(values * values, axis=-1, keepdims=True) + 1e-06)
    return (values * scaling * gain_row).astype(jnp.bfloat16)


def shards(
    residual,
    norm_gain,
    gate_weight,
    up_weight,
    down_weight,
    enc_weight,
    enc_bias,
    dec_weight,
    dec_bias,
):
    highest = lax.Precision.HIGHEST
    source = lax.axis_index("layer")
    parity = lax.axis_index("par")
    slot_count = dec_weight.shape[2]
    normed = rms_normed(residual[0], norm_gain[0])
    tokens, model_width = normed.shape
    gate_value = jnp.dot(normed, gate_weight[0], preferred_element_type=jnp.float32)
    up_value = jnp.dot(normed, up_weight[0], preferred_element_type=jnp.float32)
    hidden = (jax.nn.gelu(gate_value, approximate=True) * up_value).astype(jnp.bfloat16)
    target_part = jnp.dot(hidden, down_weight[0], preferred_element_type=jnp.float32)
    half_width = enc_weight.shape[1]
    my_rows = lax.dynamic_slice_in_dim(normed, parity * half_width, half_width, 1).astype(
        jnp.float32
    )
    pre_part = jnp.dot(my_rows, enc_weight[0], precision=highest)
    pre_act = lax.psum(pre_part, "par") + enc_bias[0]
    positive = jnp.maximum(pre_act, 0.0)
    actives = (positive * positive).astype(jnp.bfloat16)
    slot_ids = jnp.arange(slot_count, dtype=jnp.int32)
    slot_live = 2 * slot_ids + parity >= source
    live_float = slot_live.astype(jnp.float32)
    decoders = dec_weight[0, 0]
    recon_parts = (
        jnp.einsum("tf,jfd->jtd", actives, decoders, preferred_element_type=jnp.float32)
        * live_float[:, None, None]
    )
    bias_slots = lax.dynamic_index_in_dim(
        dec_bias.reshape(slot_count, 2, model_width), parity, 1, keepdims=False
    )
    partner = partner_2(target_part, "par", 0)
    own_slot = ((slot_ids == source // 2) & (source % 2 == parity)).astype(jnp.float32)
    contrib = recon_parts - own_slot[:, None, None] * (target_part + partner)[None]
    summed_rows = lax.psum(contrib, ("layer", "feat"))
    err_full = summed_rows + bias_slots[:, None, :]
    errors = (err_full * 0.0625).astype(jnp.bfloat16)
    masked = errors * slot_live.astype(jnp.bfloat16)[:, None, None]
    back_part = jnp.einsum("jtd,jfd->tf", masked, decoders, preferred_element_type=jnp.float32)
    back_grad = lax.psum(back_part.astype(jnp.bfloat16), "par").astype(jnp.float32)
    d_pre = back_grad * 2.0 * positive
    enc_grad = lax.dot_general(my_rows, d_pre, (((0,), (0,)), ((), ())), precision=highest)
    bias_grad = jnp.sum(d_pre, axis=0)
    dec_grad = jnp.einsum(
        "tf,jtd->jfd", actives, masked, preferred_element_type=jnp.float32
    ).astype(jnp.bfloat16)
    return (enc_grad[None], bias_grad[None], dec_grad[None, None])


def solution(mesh):
    return jax.shard_map(
        shards,
        mesh=mesh,
        in_specs=(
            P("layer", None, None),
            P("layer", None),
            P("layer", None, ("feat", "par")),
            P("layer", None, ("feat", "par")),
            P("layer", ("feat", "par"), None),
            P("layer", "par", "feat"),
            P("layer", "feat"),
            P("layer", "par", None, "feat", None),
            P(),
        ),
        out_specs=(
            P("layer", "par", "feat"),
            P("layer", "feat"),
            P("layer", "par", None, "feat", None),
        ),
        check_vma=False,
    )
```

profile of v0, /device:TPU:0, one launch (start us, length us, event | category | flops | bytes accessed | tf_op | source)
XLA Modules:
  0.0 536.0 jit_solution(9293100787863199491)
XLA Ops:
  7.2 0.0 all-reduce.4.cloned.1.call-start
  7.2 2.2 multiply_reduce_fusion
  9.4 0.7 reduce
  10.2 0.0 copy-start
  10.2 8.3 %fusion.29 = f32[512,1152]{1,0:T(8,128)} fusion(bf16[1,2304,1152]{2,1,0:T(8,128)(2,1)} %param.11, bf16[1,512,2304]{2,1,0:T(8,128)(2,1)} %param.9, f32[2304]{0:T(1024)S(1)} %reduce, f32[512]{0:T(512)S(1)} %add_rsqrt_fusion), kind=kOutput, calls=%fused_computation.35 | convolution fusion | flops 2727346176 | bytes 10038272 | tf_op jit(solution)/shard_map/dot_general | solution.py:36
  18.4 0.0 copy-done
  18.4 13.4 %fusion.6 = f32[512,2304]{1,0:T(8,128)} fusion(bf16[1,1152,2304]{2,1,0:T(8,128)(2,1)} %param.13, f32[512,1152]{1,0:T(8,128)} %fusion.29, bf16[1,2304,1152]{2,1,0:T(8,128)(2,1)} %param.12, bf16[1,512,2304]{2,1,0:T(8,128)(2,1)S(1)} %copy-done, f32[2304]{0:T(1024)S(1)} %reduce, f32[512]{0:T(512)S(1)} %add_rsqrt_fusion), kind=kOutput, calls=%fused_computation.12 | convolution fusion | flops 5441716224 | bytes 20065280 | tf_op jit(solution)/shard_map/dot_general | solution.py:39
  31.8 3.0 collective-permute-start
  34.8 2.5 convert_bitcast_fusion.1
  37.3 0.1 dynamic-slice
  37.4 13.5 %fusion.4 = f32[512,2048]{1,0:T(8,128)} fusion(f32[1,1152,2048]{2,1,0:T(8,128)} %param.14, f32[512,2304]{1,0:T(8,128)} %convert_bitcast_fusion.1, s32[]{:T(128)S(6)} %select_n.18, f32[1152]{0:T(1024)S(1)} %dynamic-slice, f32[512]{0:T(512)S(1)} %add_rsqrt_fusion), kind=kOutput, calls=%fused_computation.6 | convolution fusion | flops 14497284096 | bytes 15997444 | tf_op jit(solution)/shard_map/dot_general | solution.py:44
  50.9 0.0 all-reduce.4.cloned.1.call-update
  50.9 0.0 all-reduce.6.cloned.1.call-start
  51.0 0.0 copy-start.4
  51.0 155.3 %collective-permute-done = f32[512,2304]{1,0:T(8,128)} collective-permute-done((f32[512,2304]{1,0:T(8,128)}, f32[512,2304]{1,0:T(8,128)}, u32[]{:S(2)}, u32[]{:S(2)}) %collective-permute-start) | collective-permute-done | bytes 4718624 | tf_op jit(solution)/shard_map/ppermute | solution.py:10
  206.3 6.5 %add.86 = f32[512,2304]{1,0:T(8,128)} add(f32[512,2304]{1,0:T(8,128)} %fusion.6, f32[512,2304]{1,0:T(8,128)} %collective-permute-done) | non-fusion elementwise | flops 1179648 | bytes 14155776 | tf_op jit(solution)/shard_map/add | solution.py:61
  212.8 14.1 %all-reduce.4.cloned.1.call-done = f32[512,2048]{1,0:T(8,128)} async-done(((f32[512,2048]{1,0:T(8,128)}), f32[512,2048]{1,0:T(8,128)}) %all-reduce.4.cloned.1.call-update) | async-done | bytes 4194320 | tf_op jit(solution)/shard_map/psum | solution.py:45
  226.9 0.0 copy-done.4
  226.9 18.0 %bitcast_subtract_fusion = f32[2,512,2304]{2,1,0:T(8,128)} fusion(f32[512,2304]{1,0:T(8,128)} %add.86, f32[2]{0:T(128)S(1)} %get-tuple-element.6, f32[2]{0:T(128)S(1)} %get-tuple-element.7, bf16[1,1,2,2048,2304]{4,3,2,1,0:T(8,128)(2,1)} %param.16, f32[512,2048]{1,0:T(8,128)} %all-reduce.4.cloned.1.call-done, f32[2048]{0:T(1024)S(1)} %bitcast.61), kind=kOutput, calls=%fused_computation.5 | convolution fusion | flops 9674948608 | bytes 37232656 | tf_op jit(solution)/shard_map/tf,jfd->jtd/dot_general | solution.py:53
  244.9 0.0 copy-start.3
  244.9 0.0 all-reduce.6.cloned.1.call-update
  245.0 0.0 all-reduce.8.cloned.1.call-start
  245.0 0.7 copy-done.3
  245.8 185.5 %all-reduce.6.cloned.1.call-done = f32[2,512,2304]{2,1,0:T(8,128)} async-done(((f32[2,512,2304]{2,1,0:T(8,128)}), f32[2,512,2304]{2,1,0:T(8,128)}) %all-reduce.6.cloned.1.call-update) | async-done | bytes 9437200 | tf_op jit(solution)/shard_map/psum | solution.py:62
  431.3 17.5 %bitcast_convert_fusion = bf16[512,2048]{1,0:T(8,128)(2,1)} fusion(bf16[1,1,2,2048,2304]{4,3,2,1,0:T(8,128)(2,1)} %param.16, f32[2,512,2304]{2,1,0:T(8,128)} %all-reduce.6.cloned.1.call-done, f32[2,2304]{1,0:T(2,128)S(1)} %bitcast.59, bf16[2]{0:T(256)(128)(2,1)S(1)} %compare_convert_fusion), kind=kOutput, calls=%fused_computation.22 | convolution fusion | flops 9674162176 | bytes 30427140 | tf_op jit(solution)/shard_map/jtd,jfd->tf/dot_general | solution.py:66
  448.8 0.0 all-reduce.8.cloned.1.call-update
  448.8 17.7 %convert_bitcast_fusion = bf16[1,1,2,2048,2304]{3,4,2,1,0:T(8,128)(2,1)} fusion(f32[512,2048]{1,0:T(8,128)} %all-reduce.4.cloned.1.call-done, f32[2048]{0:T(1024)S(1)} %bitcast.62, f32[2,512,2304]{2,1,0:T(8,128)} %all-reduce.6.cloned.1.call-done, f32[2,2304]{1,0:T(2,128)S(1)} %bitcast.60, bf16[2]{0:T(256)(128)(2,1)S(1)} %compare_convert_fusion), kind=kOutput, calls=%fused_computation.4 | convolution fusion | flops 9686745088 | bytes 32532484 | tf_op jit(solution)/shard_map/tf,jtd->jfd/dot_general | solution.py:71
  466.5 24.8 %copy.13 = bf16[1,1,2,2048,2304]{4,3,2,1,0:T(8,128)(2,1)} copy(bf16[1,1,2,2048,2304]{3,4,2,1,0:T(8,128)(2,1)} %convert_bitcast_fusion) | data formatting | bytes 37748736
  491.2 20.8 %all-reduce.8.cloned.1.call-done = bf16[512,2048]{1,0:T(8,128)(2,1)} async-done(((bf16[512,2048]{1,0:T(8,128)(2,1)}), bf16[512,2048]{1,0:T(8,128)(2,1)}) %all-reduce.8.cloned.1.call-update) | async-done | bytes 2097168 | tf_op jit(solution)/shard_map/psum | solution.py:67
  512.0 0.0 copy-start.1
  512.0 0.0 copy-start.2
  512.0 4.5 fusion.35
  516.5 0.0 copy-done.1
  516.5 0.3 copy-done.2
  516.7 12.7 %convolution_bitcast_fusion = f32[1,1152,2048]{2,1,0:T(8,128)} fusion(bf16[512,2048]{1,0:T(8,128)(2,1)S(1)} %copy-done.2, f32[512,2048]{1,0:T(8,128)S(1)} %copy-done.1, f32[2048]{0:T(1024)S(1)} %bitcast.64, f32[512,2304]{1,0:T(8,128)} %convert_bitcast_fusion.1, s32[]{:T(128)S(6)} %select_n.18, f32[1152]{0:T(1024)S(1)} %dynamic-slice, f32[512]{0:T(512)S(1)} %add_rsqrt_fusion), kind=kOutput, calls=%fused_computation.9 | convolution fusion | flops 14502526976 | bytes 18102788 | tf_op jit(solution)/shard_map/dot_general | solution.py:69
  (6 shorter events, 0.1 us)
Async XLA Ops:
  7.2 219.8 %all-reduce.4.cloned.1.call-start = ((), (), s32[]{:S(2)}) async-start(), calls=%async_computation | async-start | bytes 8388608 | tf_op jit(solution)/shard_map/psum | solution.py:45
  10.2 8.3 %copy-start = (bf16[1,512,2304]{2,1,0:T(8,128)(2,1)S(1)}, bf16[1,512,2304]{2,1,0:T(8,128)(2,1)}, u32[]{:S(2)}) copy-start(bf16[1,512,2304]{2,1,0:T(8,128)(2,1)} %param.9) | copy-start | bytes 7077892
  31.8 174.5 %collective-permute-start = (f32[512,2304]{1,0:T(8,128)}, f32[512,2304]{1,0:T(8,128)}, u32[]{:S(2)}, u32[]{:S(2)}) collective-permute-start(f32[512,2304]{1,0:T(8,128)} %fusion.6), channel_id=1, source_target_pairs={{0,1},{1,0},{2,3},{3,2},{4,5},{5,4},{6,7},{7,6},{8,9},{9,8},{10,11... | collective-permute-start | bytes 14155784 | tf_op jit(solution)/shard_map/ppermute | solution.py:10
  50.9 380.4 %all-reduce.6.cloned.1.call-start = ((), (), s32[]{:S(2)}) async-start(), calls=%async_computation.1 | async-start | bytes 18874368 | tf_op jit(solution)/shard_map/psum | solution.py:62
  51.0 176.0 %copy-start.4 = (f32[1,2048]{1,0:T(1,128)S(1)}, f32[1,2048]{1,0:T(1,128)}, u32[]{:S(2)}) copy-start(f32[1,2048]{1,0:T(1,128)} %param.15) | copy-start | bytes 24580
  244.9 0.8 copy-start.3
  245.0 267.1 %all-reduce.8.cloned.1.call-start = ((), (), s32[]{:S(2)}) async-start(), calls=%async_computation.2 | async-start | bytes 4194304 | tf_op jit(solution)/shard_map/psum | solution.py:67
  512.0 4.5 copy-start.1
  512.0 4.7 copy-start.2
Sparse Core Ops, SparseCore 0:
  51.0 175.8 all-reduce.3
  245.1 186.1 all-reduce.5
  448.9 63.0 all-reduce.7
where the time goes:
time: 537 us; the launch traced here: 536 us
  waiting for transfers between devices  376 us (70%)
  matrix products  101 us (19%)
  local copies, waits for them, and re-layouts  25.9 us (5%)
  other arithmetic  16.4 us (3%)
  between operations  13.8 us (3%)
    psum x1, waiting for transfers between devices, shards(): summed_rows = lax.psum(contrib, ('layer', 'feat'))  185 us
    ppermute x1, waiting for transfers between devices, partner_2(): return lax.ppermute(value, axis, pairs)  155 us
    unnamed x12, local copies, waits for them, and re-layouts  25.8 us
    psum x1, waiting for transfers between devices, shards(): lax.psum(back_part.astype(jnp.bfloat16), 'par').astype(jnp.float32)  20.8 us
    dot_general x1, matrix products, shards(): jnp.einsum('tf,jfd->jtd', actives, decoders, preferred_element_type=jnp.f...  18 us
    dot_general x1, matrix products, shards(): jnp.einsum('tf,jtd->jfd', actives, masked, preferred_element_type=jnp.flo...  17.7 us
    dot_general x1, matrix products, shards(): jnp.einsum('jtd,jfd->tf', masked, decoders, preferred_element_type=jnp.fl...  17.5 us
    psum x1, waiting for transfers between devices, shards(): pre_act = lax.psum(pre_part, 'par') + enc_bias[0]  14.1 us
  transfers between devices with their start and end apart: 4, of which 4 were waited for; matrix products, arithmetic and copies ran while one was open for 12% of the time, Pallas kernels for 0%

commit v1 on v0

v1 whole, which is shorter than its diff:
```python
import functools

import jax
import jax.numpy as jnp
from jax import lax
from jax.experimental import pallas as pl
from jax.experimental.pallas import tpu as pltpu
from jax.sharding import PartitionSpec as P


CHUNKS = 2
F32 = jnp.float32
BF16 = jnp.bfloat16
LIMITS = pltpu.CompilerParams(vmem_limit_bytes=46 * 2**20)


def tile_of(size, limit):
    best = size
    for tile in range(128, min(size, limit) + 1, 128):
        if size % tile == 0:
            best = tile
    return best


def positive_of(own, moved, bias):
    return jnp.maximum(own.astype(F32) + moved.astype(F32) + bias, 0.0)


def tied(value, *first):
    return lax.optimization_barrier((value, *first))[0]


def product(left, right, left_dim, right_dim):
    return lax.dot_general(
        left, right, (((left_dim,), (right_dim,)), ((), ())), preferred_element_type=F32
    )


def encode_body(place_ref, rows_ref, gain_ref, weight_ref, normed_ref, *rest):
    send_refs, half_ref = rest[:-1], rest[-1]
    blocks = place_ref.shape[0] - 1
    tokens, half = half_ref.shape
    size = tokens // blocks

    @pl.when(pl.program_id(0) == 0)
    def _():
        column = pl.multiple_of(place_ref[blocks] * half, 128)
        for b in range(blocks):
            start = pl.multiple_of(place_ref[b] * size, size)
            values = rows_ref[pl.ds(start, size), :].astype(F32)
            scaling = lax.rsqrt(jnp.mean(values * values, axis=-1, keepdims=True) + 1e-06)
            kept = slice(b * size, (b + 1) * size)
            normed_ref[kept, :] = (values * scaling * gain_ref[...]).astype(BF16)
            half_ref[kept, :] = normed_ref[kept, pl.ds(column, half)]

    part = product(half_ref[...], weight_ref[...].astype(BF16), 1, 0)
    span = tokens // len(send_refs)
    for c, send_ref in enumerate(send_refs):
        send_ref[...] = part[c * span : (c + 1) * span].astype(BF16)


def encode(place, rows, gain, weight):
    tokens, width = rows.shape
    half, feats = weight.shape
    tile = tile_of(feats, 512)
    size = tokens // CHUNKS
    return pl.pallas_call(
        encode_body,
        grid_spec=pltpu.PrefetchScalarGridSpec(
            num_scalar_prefetch=1,
            grid=(feats // tile,),
            in_specs=[
                pl.BlockSpec((tokens, width), lambda f, place: (0, 0)),
                pl.BlockSpec((1, width), lambda f, place: (0, 0)),
                pl.BlockSpec((half, tile), lambda f, place: (0, f)),
            ],
            out_specs=[pl.BlockSpec((tokens, width), lambda f, place: (0, 0))]
            + [pl.BlockSpec((size, tile), lambda f, place: (0, f))] * CHUNKS,
            scratch_shapes=[pltpu.VMEM((tokens, half), BF16)],
        ),
        out_shape=[jax.ShapeDtypeStruct((tokens, width), BF16)]
        + [jax.ShapeDtypeStruct((size, feats), BF16)] * CHUNKS,
        name="encode",
    )(place, rows, gain, weight)


def mlp_body(k_steps, rows_ref, gate_ref, up_ref, down_ref, out_ref, gate_acc, up_acc, hidden):
    step = pl.program_id(0)

    @pl.when(step == 0)
    def _():
        gate_acc[...] = product(rows_ref[...], gate_ref[...], 1, 0)
        up_acc[...] = product(rows_ref[...], up_ref[...], 1, 0)

    @pl.when((step > 0) & (step < k_steps))
    def _():
        gate_acc[...] += product(rows_ref[...], gate_ref[...], 1, 0)
        up_acc[...] += product(rows_ref[...], up_ref[...], 1, 0)

    @pl.when(step == k_steps - 1)
    def _():
        hidden[...] = (jax.nn.gelu(gate_acc[...], approximate=True) * up_acc[...]).astype(BF16)

    @pl.when(step >= k_steps)
    def _():
        out_ref[...] = product(hidden[...], down_ref[...], 1, 0).astype(BF16)


def mlp(normed, gate, up, down):
    tokens, width = normed.shape
    inner = gate.shape[1]
    tile = tile_of(width, 768)
    steps = width // tile
    early = lambda i: jnp.minimum(i, steps - 1)
    late = lambda i: jnp.maximum(i - steps, 0)
    return pl.pallas_call(
        functools.partial(mlp_body, steps),
        grid=(2 * steps,),
        in_specs=[
            pl.BlockSpec((tokens, tile), lambda i: (0, early(i))),
            pl.BlockSpec((tile, inner), lambda i: (early(i), 0)),
            pl.BlockSpec((tile, inner), lambda i: (early(i), 0)),
            pl.BlockSpec((inner, tile), lambda i: (0, late(i))),
        ],
        out_specs=pl.BlockSpec((tokens, tile), lambda i: (0, late(i))),
        out_shape=jax.ShapeDtypeStruct((tokens, width), BF16),
        scratch_shapes=[
            pltpu.VMEM((tokens, inner), F32),
            pltpu.VMEM((tokens, inner), F32),
            pltpu.VMEM((tokens, inner), BF16),
        ],
        name="mlp",
    )(normed, gate, up, down)


def decode_body(
    flags_ref, own_ref, moved_ref, bias_ref, weight_ref, target_ref, act_ref, keep_ref, send_ref
):
    slot = pl.program_id(0)
    slots = pl.num_programs(0)

    @pl.when((slot == 0) & (pl.program_id(1) == 0))
    def _():
        positive = positive_of(own_ref[...], moved_ref[...], bias_ref[...])
        act_ref[...] = (positive * positive).astype(BF16)

    live = flags_ref[slot].astype(F32)
    mine = flags_ref[slots + slot].astype(F32)
    recon = product(act_ref[...], weight_ref[0], 1, 0) * live
    recon = recon - target_ref[...].astype(F32) * mine
    half = recon.shape[0] // 2
    keep_ref[0] = recon[:half]
    send_ref[0] = recon[half:].astype(BF16)


def decode(flags, own, moved, bias, decoders, target, chunk):
    size, feats = own.shape
    slots, _, width = decoders.shape
    tile = tile_of(width, 768)
    whole = pl.BlockSpec((size, feats), lambda j, d, flags: (0, 0))
    part = pl.BlockSpec((1, size // 2, tile), lambda j, d, flags: (j, 0, d))
    return pl.pallas_call(
        decode_body,
        grid_spec=pltpu.PrefetchScalarGridSpec(
            num_scalar_prefetch=1,
            grid=(slots, width // tile),
            in_specs=[
                whole,
                whole,
                pl.BlockSpec((1, feats), lambda j, d, flags: (0, 0)),
                pl.BlockSpec((1, feats, tile), lambda j, d, flags: (j, 0, d)),
                pl.BlockSpec((size, tile), lambda j, d, flags: (chunk, d)),
            ],
            out_specs=[whole, part, part],
        ),
        out_shape=[
            jax.ShapeDtypeStruct((size, feats), BF16),
            jax.ShapeDtypeStruct((slots, size // 2, width), F32),
            jax.ShapeDtypeStruct((slots, size // 2, width), BF16),
        ],
        compiler_params=LIMITS,
        name="decode",
    )(flags, own, moved, bias, decoders, target)


def back_body(err_ref, weight_ref, part_ref, send_ref):
    part = product(err_ref[0], weight_ref[0], 1, 1)
    for j in range(1, err_ref.shape[0]):
        part = part + product(err_ref[j], weight_ref[j], 1, 1)
    part_ref[...] = part
    send_ref[...] = part.astype(BF16)


def back_product(errors, decoders):
    slots, size, width = errors.shape
    feats = decoders.shape[1]
    tile = tile_of(feats, 512)
    return pl.pallas_call(
        back_body,
        grid=(feats // tile,),
        in_specs=[
            pl.BlockSpec((slots, size, width), lambda f: (0, 0, 0)),
            pl.BlockSpec((slots, tile, width), lambda f: (0, f, 0)),
        ],
        out_specs=[
            pl.BlockSpec((size, tile), lambda f: (0, f)),
            pl.BlockSpec((size, tile), lambda f: (0, f)),
        ],
        out_shape=[
            jax.ShapeDtypeStruct((size, feats), F32),
            jax.ShapeDtypeStruct((size, feats), BF16),
        ],
        compiler_params=LIMITS,
        name="back_product",
    )(errors, decoders)


def dec_grad_body(*refs):
    acts, errs, out_ref = refs[:CHUNKS], refs[CHUNKS : 2 * CHUNKS], refs[-1]
    turned = [act_ref[...].T for act_ref in acts]
    for j in range(out_ref.shape[0]):
        total = product(turned[0], errs[0][j], 1, 0)
        for c in range(1, CHUNKS):
            total = total + product(turned[c], errs[c][j], 1, 0)
        out_ref[j] = total.astype(BF16)


def dec_grad_product(actives, errors):
    size, feats = actives[0].shape
    slots, _, width = errors[0].shape
    tile = tile_of(feats, 256)
    return pl.pallas_call(
        dec_grad_body,
        grid=(feats // tile,),
        in_specs=[pl.BlockSpec((size, tile), lambda f: (0, f))] * CHUNKS
        + [pl.BlockSpec((slots, size, width), lambda f: (0, 0, 0))] * CHUNKS,
        out_specs=pl.BlockSpec((slots, tile, width), lambda f: (0, f, 0)),
        out_shape=jax.ShapeDtypeStruct((slots, feats, width), BF16),
        compiler_params=LIMITS,
        name="dec_grad",
    )(*actives, *errors)


def enc_grad_body(parity_ref, rows_ref, bias_in_ref, *refs):
    parts, moved, own, seen = (refs[i * CHUNKS : (i + 1) * CHUNKS] for i in range(4))
    grad_ref, bias_ref = refs[-2:]
    grads = []
    bias = 0.0
    for c in range(CHUNKS):
        positive = positive_of(own[c][...], seen[c][...], bias_in_ref[...])
        d_pre = (parts[c][...] + moved[c][...].astype(F32)) * 2.0 * positive
        bias = bias + jnp.sum(d_pre, axis=0, keepdims=True)
        grads.append(d_pre.astype(BF16))
    bias_ref[...] = bias
    grad_ref[...] = product(rows_ref[...], jnp.concatenate(grads, axis=0), 0, 0)


def enc_grad_product(parity, normed, half, bias, parts, moved, own, seen):
    tokens = normed.shape[0]
    size, feats = parts[0].shape
    tile = tile_of(feats, 512)
    return pl.pallas_call(
        enc_grad_body,
        grid_spec=pltpu.PrefetchScalarGridSpec(
            num_scalar_prefetch=1,
            grid=(feats // tile,),
            in_specs=[
                pl.BlockSpec((tokens, half), lambda f, par: (0, par[0])),
                pl.BlockSpec((1, tile), lambda f, par: (0, f)),
            ]
            + [pl.BlockSpec((size, tile), lambda f, par: (0, f))] * (4 * CHUNKS),
            out_specs=[
                pl.BlockSpec((half, tile), lambda f, par: (0, f)),
                pl.BlockSpec((1, tile), lambda f, par: (0, f)),
            ],
        ),
        out_shape=[
            jax.ShapeDtypeStruct((half, feats), F32),
            jax.ShapeDtypeStruct((1, feats), F32),
        ],
        compiler_params=LIMITS,
        name="enc_grad",
    )(parity, normed, bias, *parts, *moved, *own, *seen)


def shards(
    residual,
    norm_gain,
    gate_weight,
    up_weight,
    down_weight,
    enc_weight,
    enc_bias,
    dec_weight,
    dec_bias,
):
    layers = lax.axis_size("layer")
    feat_n = lax.axis_size("feat")
    outer = layers // 2
    source = lax.axis_index("layer")
    parity = lax.axis_index("par")
    slots = dec_weight.shape[2]
    _, tokens, width = residual.shape
    half_width = enc_weight.shape[1]
    size = tokens // CHUNKS
    rows_n = size // (layers * feat_n)

    def over_par(value):
        return lax.ppermute(value, "par", [(0, 1), (1, 0)])

    def over_layer(value, mask):
        return lax.ppermute(value, "layer", [(s, s ^ mask) for s in range(layers)])

    def over_feat(value):
        return lax.all_to_all(value, "feat", 0, 0, tiled=True)

    index = jnp.arange(CHUNKS * layers, dtype=jnp.int32)
    table = index ^ (source % 2 * outer + source // 2)
    parity_arg = jnp.full((1,), parity, jnp.int32)
    place = jnp.concatenate([table, parity_arg])
    normed, *pre_send = encode(place, residual[0], norm_gain, enc_weight[0])
    pre_moved = []
    for c in range(CHUNKS):
        pre_moved.append(over_par(pre_send[c]))
    target_part = mlp(normed, gate_weight[0], up_weight[0], down_weight[0])

    pairs = [(s * 2 + 1 - s % 2, (s ^ 1) * 2 + 1 - s % 2) for s in range(layers)]
    halves = target_part.reshape(CHUNKS, 2, outer, feat_n, rows_n, width)
    handed = lax.ppermute(halves[:, 1], ("layer", "par"), pairs)
    moving = jnp.where(source % 2 == parity, handed, halves[:, 0])
    moving = moving.transpose(2, 0, 1, 3, 4)
    target_moved = over_feat(moving)

    slot_ids = jnp.arange(slots, dtype=jnp.int32)
    decoders = dec_weight[0, 0]
    live = 2 * slot_ids + parity >= source
    mine = (slot_ids == source // 2) & (source % 2 == parity)
    flags = jnp.concatenate([live, mine]).astype(jnp.int32)
    bias_rows = lax.dynamic_index_in_dim(
        dec_bias.reshape(slots, 2, width), parity, 1, keepdims=False
    )

    actives = []
    wholes = []
    last = moving
    for c in range(CHUNKS):
        active, keep, send = decode(
            flags, pre_send[c], tied(pre_moved[c], last), enc_bias, decoders, target_part, c
        )
        actives.append(active)
        got = over_layer(send, 1)
        both = (keep + got.astype(F32)).reshape(slots, outer, feat_n * rows_n, width)
        whole = both[:, 0]
        for high in range(1, outer):
            last = both[:, high].astype(BF16)
            got = over_layer(last, 2 * high)
            whole = whole + got.astype(F32)
        wholes.append(whole.astype(BF16).reshape(slots, feat_n, rows_n, width).swapaxes(0, 1))

    summed = jnp.sum(tied(target_moved, last).astype(F32), axis=0)
    crossed = over_par(summed.astype(BF16).transpose(1, 0, 2, 3))
    far_target = 0.0
    for high in range(outer):
        got = crossed[0] if high == 0 else over_layer(crossed[high], 2 * high)
        chosen = slot_ids == ((source // 2) ^ high)
        far_target = far_target + jnp.where(
            chosen[:, None, None, None], got[None].astype(F32), 0.0
        )

    gathered = []
    for c in range(CHUNKS):
        got = over_feat(wholes[c])
        if c:
            got = tied(got, error)
        total = jnp.sum(got.astype(F32), axis=0)
        error = (total - far_target[:, c] + bias_rows[:, None]) * 0.0625
        error = error.astype(BF16)
        gathered.append(over_feat(jnp.broadcast_to(error[None], (feat_n,) + error.shape)))

    errors = []
    parts = []
    moved = []
    for c in range(CHUNKS):
        rows = [gathered[c]]
        for high in range(1, outer):
            rows.append(over_layer(gathered[c], 2 * high))
        rows = jnp.stack(rows)
        other = over_layer(rows, 1)
        if c:
            rows, other = lax.optimization_barrier((rows, other, parts[-1]))[:2]
        rows = jnp.stack([rows, other])
        rows = rows.transpose(3, 0, 1, 2, 4, 5).reshape(slots, size, width)
        errors.append(jnp.where(live[:, None, None], rows, jnp.zeros_like(rows)))
        part, send = back_product(errors[c], decoders)
        parts.append(part)
        moved.append(over_par(send))
    dec_grad = dec_grad_product(actives, errors[:-1] + [tied(errors[-1], send)])
    enc_grad, bias_grad = enc_grad_product(
        parity_arg, normed, half_width, enc_bias, parts, moved, pre_send, pre_moved
    )
    return (enc_grad[None], bias_grad, dec_grad[None, None])


def solution(mesh):
    return jax.shard_map(
        shards,
        mesh=mesh,
        in_specs=(
            P("layer", None, None),
            P("layer", None),
            P("layer", None, ("feat", "par")),
            P("layer", None, ("feat", "par")),
            P("layer", ("feat", "par"), None),
            P("layer", "par", "feat"),
            P("layer", "feat"),
            P("layer", "par", None, "feat", None),
            P(),
        ),
        out_specs=(
            P("layer", "par", "feat"),
            P("layer", "feat"),
            P("layer", "par", None, "feat", None),
        ),
        check_vma=False,
    )
```

time: 537 us -> 318 us (0.59)
  waiting for transfers between devices: 376 us -> 135 us
  matrix products: 101 us -> 0 us
  Pallas kernels: 0 us -> 89.5 us
  starting transfers between devices: 3.13 us -> 34.8 us
  blocking collectives: 0 us -> 16.9 us
  between operations: 13.8 us -> 0.96 us
  local copies, waits for them, and re-layouts: 25.9 us -> 15.9 us
  other arithmetic: 16.4 us -> 24.5 us
    psum x3 -> x0, waiting for transfers between devices: 220 us -> none  [the longest x1 185 us: shards(): summed_rows = lax.psum(contrib, ('layer', 'feat'))]
    dot_general x7 -> x0, matrix products: 101 us -> none  [the longest x1 18 us: shards(): jnp.einsum('tf,jfd->jtd', actives, decoders, preferred_element_type=jnp.f...]
    pallas_call x0 -> x8, Pallas kernels: none -> 89.5 us  [the longest x2 23.7 us: decode(): pl.pallas_call(decode_body, grid_spec=pltpu.PrefetchScalarGridSpec(num_sc...]
    ppermute x1 -> x15, waiting for transfers between devices: 155 us -> 98.6 us  [the longest x5 62.8 us: over_par(): return lax.ppermute(value, 'par', [(0, 1), (1, 0)])]
    all_to_all x0 -> x4, waiting for transfers between devices: none -> 36.1 us  [over_feat(): return lax.all_to_all(value, 'feat', 0, 0, tiled=True)]
    all_to_all x0 -> x4, starting transfers between devices: none -> 19 us  [over_feat(): return lax.all_to_all(value, 'feat', 0, 0, tiled=True)]
    unnamed x12 -> x34, local copies, waits for them, and re-layouts: 25.8 us -> 8.06 us
    all_to_all x0 -> x1, blocking collectives: none -> 16.9 us  [over_feat(): return lax.all_to_all(value, 'feat', 0, 0, tiled=True)]
  transfers between devices with their start and end apart: 4 -> 19, of which waited for: 4 -> 11; matrix products, arithmetic and copies ran while one was open for 12% -> 8% of each run, Pallas kernels for 0% -> 10%
where the time goes in v1:
time: 318 us; the launch traced here: 317 us
  waiting for transfers between devices  135 us (42%)
  Pallas kernels  89.5 us (28%)
  starting transfers between devices  34.8 us (11%)
  other arithmetic  24.5 us (8%)
  blocking collectives  16.9 us (5%)
  local copies, waits for them, and re-layouts  15.9 us (5%)
    ppermute x5, waiting for transfers between devices, over_par(): return lax.ppermute(value, 'par', [(0, 1), (1, 0)])  62.8 us
    all_to_all x4, waiting for transfers between devices, over_feat(): return lax.all_to_all(value, 'feat', 0, 0, tiled=True)  36.1 us
    ppermute x9, waiting for transfers between devices, over_layer(): return lax.ppermute(value, 'layer', [(s, s ^ mask) for s in range(layers)])  35.9 us
    pallas_call x2, Pallas kernels, decode(): pl.pallas_call(decode_body, grid_spec=pltpu.PrefetchScalarGridSpec(num_sc...  23.7 us
    all_to_all x4, starting transfers between devices, over_feat(): return lax.all_to_all(value, 'feat', 0, 0, tiled=True)  19 us
    pallas_call x2, Pallas kernels, back_product(): pl.pallas_call(back_body, grid=(feats // tile,), in_specs=[pl.BlockSpec((...  18.6 us
    all_to_all x1, blocking collectives, over_feat(): return lax.all_to_all(value, 'feat', 0, 0, tiled=True)  16.9 us
    pallas_call x1, Pallas kernels, mlp(): pl.pallas_call(functools.partial(mlp_body, steps), grid=(2 * steps,), in_...  15.5 us
  transfers between devices with their start and end apart: 19, of which 11 were waited for; matrix products, arithmetic and copies ran while one was open for 8% of the time, Pallas kernels for 10%

profile of v1, /device:TPU:0, one launch (start us, length us, event | category | flops | bytes accessed | tf_op | source)
XLA Modules:
  0.0 317.2 jit_solution(15800850311283477371)
XLA Ops:
  0.7 0.6 pad_add_fusion.place_ref
  1.3 10.2 %encode.1 = (bf16[512,2304]{1,0:T(8,128)(2,1)}, bf16[256,2048]{1,0:T(8,128)(2,1)}, bf16[256,2048]{1,0:T(8,128)(2,1)}) custom-call(s32[9]{0:T(128)} %pad_add_fusion.place_ref, bf16[512,2304]{1,0:T(8,128)(2,1)} %bitcast.110, f32[1,2304]{1,0:T(1,128)} %gain_ref.1, f32[1152,2048]{1,0:T(8,128)} %bitcast.99), custom_call_target="tpu_custom_call" | custom-call | tf_op jit(solution)/shard_map/encode/pallas_call | solution.py:67
  11.4 15.5 %mlp.1.target_ref = bf16[512,2304]{1,0:T(8,128)(2,1)} custom-call(bf16[512,2304]{1,0:T(8,128)(2,1)} %get-tuple-element.24.rows_ref, bf16[2304,1152]{1,0:T(8,128)(2,1)} %bitcast.104, bf16[2304,1152]{1,0:T(8,128)(2,1)} %bitcast.105, bf16[1152,2304]{1,0:T(8,128)(2,1)} %bitcast.106), custom_call_target="tpu_custom_call" | custom-call | tf_op jit(solution)/shard_map/mlp/pallas_call | solution.py:116
  26.9 2.8 fusion.18
  29.8 1.1 copy.68
  30.9 1.4 collective-permute-start.1
  32.3 4.5 %collective-permute-start = (bf16[256,2048]{1,0:T(8,128)(2,1)S(1)}, bf16[256,2048]{1,0:T(8,128)(2,1)S(1)}, u32[]{:S(2)}, u32[]{:S(2)}) collective-permute-start(bf16[256,2048]{1,0:T(8,128)(2,1)S(1)} %copy-done), channel_id=1, source_target_pairs={{0,1},{1,0},{2,3},{3,2},{4,5},{5,4},{6,7},{7,6},{8,9},{9,8},{10,11... | collective-permute-start | bytes 3145736 | tf_op jit(solution)/shard_map/ppermute | solution.py:309
  36.9 2.8 fusion.5
  39.6 19.9 %collective-permute-done.moved_ref.refs_6_ = bf16[256,2048]{1,0:T(8,128)(2,1)S(1)} collective-permute-done((bf16[256,2048]{1,0:T(8,128)(2,1)S(1)}, bf16[256,2048]{1,0:T(8,128)(2,1)S(1)}, u32[]{:S(2)}, u32[]{:S(2)}) %collective-permute-start) | collective-permute-done | bytes 1048608 | tf_op jit(solution)/shard_map/ppermute | solution.py:309
  59.5 11.5 %decode.2 = (bf16[256,2048]{1,0:T(8,128)(2,1)S(1)}, f32[2,128,2304]{2,1,0:T(8,128)S(1)}, bf16[2,128,2304]{2,1,0:T(8,128)(2,1)S(1)}) custom-call(s32[4]{0:T(128)S(1)} %add_convert_fusion.flags_ref, bf16[256,2048]{1,0:T(8,128)(2,1)S(1)} %copy-done, bf16[256,2048]{1,0:T(8,128)(2,1)S(1)} %collective-permute-done.moved_ref.refs_6_, f32[1,2048]{1,0:T(1,128)S(1)} %copy-done.11, ...), custom_call_target="tpu_custom_call" | custom-call | tf_op jit(solution)/shard_map/decode/pallas_call | solution.py:162
  71.1 0.9 collective-permute-start.4
  71.9 2.0 collective-permute-done.2
  74.2 1.0 fusion.6
  75.1 0.6 copy-done.13
  75.7 20.9 %collective-permute-done.4.moved_ref.refs_7_ = bf16[256,2048]{1,0:T(8,128)(2,1)S(1)} collective-permute-done((bf16[256,2048]{1,0:T(8,128)(2,1)S(1)}, bf16[256,2048]{1,0:T(8,128)(2,1)S(1)}, u32[]{:S(2)}, u32[]{:S(2)}) %collective-permute-start.4) | collective-permute-done | bytes 1048608 | tf_op jit(solution)/shard_map/ppermute | solution.py:309
  96.6 12.3 %decode.3 = (bf16[256,2048]{1,0:T(8,128)(2,1)S(1)}, f32[2,128,2304]{2,1,0:T(8,128)S(1)}, bf16[2,128,2304]{2,1,0:T(8,128)(2,1)}) custom-call(s32[4]{0:T(128)S(1)} %add_convert_fusion.flags_ref, bf16[256,2048]{1,0:T(8,128)(2,1)S(1)} %copy-done.1, bf16[256,2048]{1,0:T(8,128)(2,1)S(1)} %collective-permute-done.4.moved_ref.refs_7_, f32[1,2048]{1,0:T(1,128)S(1)} %copy-done.11, ...), custom_call_target="tpu_custom_call" | custom-call | tf_op jit(solution)/shard_map/decode/pallas_call | solution.py:162
  108.9 1.4 copy-done.4
  110.3 1.0 copy-done.9
  111.3 6.0 %all-to-all-start.1 = ((bf16[4,2,2,16,2304]{4,3,2,1,0:T(8,128)(2,1)}), bf16[4,2,2,16,2304]{4,3,2,1,0:T(8,128)(2,1)}, u32[]{:S(2)}, u32[]{:S(2)}) async-start(bf16[4,2,2,16,2304]{4,3,2,1,0:T(8,128)(2,1)} %fusion.5), calls=%async_computation.1 | async-start | bytes 2359296 | tf_op jit(solution)/shard_map/all_to_all | solution.py:315
  117.3 1.6 collective-permute-start.3
  118.9 2.2 convert_add_fusion
  121.1 1.4 copy-done.12
  122.5 0.9 fusion.7
  123.4 23.2 %all-to-all-done.1 = bf16[4,2,2,16,2304]{4,3,2,1,0:T(8,128)(2,1)} async-done(((bf16[4,2,2,16,2304]{4,3,2,1,0:T(8,128)(2,1)}), bf16[4,2,2,16,2304]{4,3,2,1,0:T(8,128)(2,1)}, u32[]{:S(2)}, u32[]{:S(2)}) %all-to-all-start.1) | async-done | bytes 1179680 | tf_op jit(solution)/shard_map/all_to_all | solution.py:315
  146.6 2.2 reduce_sum.31
  148.9 0.7 collective-permute-start.6
  149.6 1.6 fusion.3
  151.1 0.9 copy.30
  152.0 4.3 %all-to-all-start = ((bf16[4,2,16,2304]{3,2,1,0:T(8,128)(2,1)}), bf16[4,2,16,2304]{3,2,1,0:T(8,128)(2,1)}, u32[]{:S(2)}, u32[]{:S(2)}) async-start(bf16[4,2,16,2304]{3,2,1,0:T(8,128)(2,1)} %copy.30), calls=%async_computation | async-start | bytes 1179648 | tf_op jit(solution)/shard_map/all_to_all | solution.py:315
  156.3 1.6 collective-permute-start.10
  157.9 0.8 fusion.16
  158.7 1.0 collective-permute-start.7
  159.7 12.8 %collective-permute-done.10 = bf16[2,64,2304]{2,1,0:T(8,128)(2,1)S(1)} collective-permute-done((bf16[2,64,2304]{2,1,0:T(8,128)(2,1)}, bf16[2,64,2304]{2,1,0:T(8,128)(2,1)S(1)}, u32[]{:S(2)}, u32[]{:S(2)}) %collective-permute-start.10) | collective-permute-done | bytes 589856 | tf_op jit(solution)/shard_map/ppermute | solution.py:312
  172.5 1.4 fusion.1
  173.9 0.9 copy.35
  174.7 4.5 %all-to-all-start.3 = ((bf16[4,2,16,2304]{3,2,1,0:T(8,128)(2,1)}), bf16[4,2,16,2304]{3,2,1,0:T(8,128)(2,1)}, u32[]{:S(2)}, u32[]{:S(2)}) async-start(bf16[4,2,16,2304]{3,2,1,0:T(8,128)(2,1)} %copy.35), calls=%async_computation.3 | async-start | bytes 1179648 | tf_op jit(solution)/shard_map/all_to_all | solution.py:315
  179.3 1.2 convert_reduce_fusion.1
  180.5 0.9 convert_element_type.64
  181.4 1.9 select_add_fusion
  183.3 8.6 %all-to-all-done.3 = bf16[4,2,16,2304]{3,2,1,0:T(8,128)(2,1)} async-done(((bf16[4,2,16,2304]{3,2,1,0:T(8,128)(2,1)}), bf16[4,2,16,2304]{3,2,1,0:T(8,128)(2,1)}, u32[]{:S(2)}, u32[]{:S(2)}) %all-to-all-start.3) | async-done | bytes 589856 | tf_op jit(solution)/shard_map/all_to_all | solution.py:315
  192.0 1.2 convert_reduce_fusion
  193.1 1.2 fusion.11
  194.4 16.9 %all_to_all.25 = bf16[4,2,16,2304]{3,2,1,0:T(8,128)(2,1)} all-to-all(bf16[4,2,16,2304]{3,2,1,0:T(8,128)(2,1)S(1)} %broadcast_in_dim.84), channel_id=1, replica_groups=mesh['layer'=4,'feat'=4,'par'=2] {'feat'}, dimensions={0} | all-to-all | bytes 1179648 | tf_op jit(solution)/shard_map/all_to_all | solution.py:315
  211.2 1.5 collective-permute-start.8
  212.7 0.9 broadcast_in_dim.85
  213.6 4.1 %all-to-all-start.4 = ((bf16[4,2,16,2304]{3,2,1,0:T(8,128)(2,1)}), bf16[4,2,16,2304]{3,2,1,0:T(8,128)(2,1)}, u32[]{:S(2)}, u32[]{:S(2)}) async-start(bf16[4,2,16,2304]{3,2,1,0:T(8,128)(2,1)} %broadcast_in_dim.85), calls=%async_computation.4 | async-start | bytes 1179648 | tf_op jit(solution)/shard_map/all_to_all | solution.py:315
  217.7 7.4 %collective-permute-done.8 = bf16[4,2,16,2304]{3,2,1,0:T(8,128)(2,1)} collective-permute-done((bf16[4,2,16,2304]{3,2,1,0:T(8,128)(2,1)}, bf16[4,2,16,2304]{3,2,1,0:T(8,128)(2,1)}, u32[]{:S(2)}, u32[]{:S(2)}) %collective-permute-start.8) | collective-permute-done | bytes 589856 | tf_op jit(solution)/shard_map/ppermute | solution.py:312
  225.1 2.8 fusion.17
  227.9 4.3 %all-to-all-done.4 = bf16[4,2,16,2304]{3,2,1,0:T(8,128)(2,1)} async-done(((bf16[4,2,16,2304]{3,2,1,0:T(8,128)(2,1)}), bf16[4,2,16,2304]{3,2,1,0:T(8,128)(2,1)}, u32[]{:S(2)}, u32[]{:S(2)}) %all-to-all-start.4) | async-done | bytes 589856 | tf_op jit(solution)/shard_map/all_to_all | solution.py:315
  232.2 0.5 collective-permute-start.11
  232.7 13.7 %collective-permute-done.11 = bf16[4,2,16,2304]{3,2,1,0:T(8,128)(2,1)S(1)} collective-permute-done((bf16[4,2,16,2304]{3,2,1,0:T(8,128)(2,1)}, bf16[4,2,16,2304]{3,2,1,0:T(8,128)(2,1)S(1)}, u32[]{:S(2)}, u32[]{:S(2)}) %collective-permute-start.11) | collective-permute-done | bytes 589856 | tf_op jit(solution)/shard_map/ppermute | solution.py:312
  246.4 1.2 pad_maximum_fusion.1
  247.7 1.5 maximum_bitcast_fusion
  249.4 0.3 bitcast_select_fusion.1.err_ref.refs_2_
  249.7 9.3 %back_product.2 = (f32[256,2048]{1,0:T(8,128)S(1)}, bf16[256,2048]{1,0:T(8,128)(2,1)S(1)}) custom-call(bf16[2,256,2304]{2,1,0:T(8,128)(2,1)S(1)} %bitcast_select_fusion.1.err_ref.refs_2_, bf16[2,2048,2304]{2,1,0:T(8,128)(2,1)} %bitcast.95), custom_call_target="tpu_custom_call" | custom-call | tf_op jit(solution)/shard_map/back_product/pallas_call | solution.py:198
  259.3 1.1 copy-done.5
  260.6 0.3 bitcast_select_fusion.err_ref.refs_3_
  260.9 1.4 collective-permute-start.13
  262.4 9.3 %back_product.3 = (f32[256,2048]{1,0:T(8,128)S(1)}, bf16[256,2048]{1,0:T(8,128)(2,1)S(1)}) custom-call(bf16[2,256,2304]{2,1,0:T(8,128)(2,1)S(1)} %bitcast_select_fusion.err_ref.refs_3_, bf16[2,2048,2304]{2,1,0:T(8,128)(2,1)} %bitcast.96), custom_call_target="tpu_custom_call" | custom-call | tf_op jit(solution)/shard_map/back_product/pallas_call | solution.py:198
  271.7 1.3 copy-done.6
  273.1 0.7 collective-permute-start.14
  273.7 13.2 %dec_grad.1 = bf16[2,2048,2304]{2,1,0:T(8,128)(2,1)} custom-call(bf16[256,2048]{1,0:T(8,128)(2,1)S(1)} %copy-done.8, bf16[256,2048]{1,0:T(8,128)(2,1)S(1)} %copy-done.10, bf16[2,256,2304]{2,1,0:T(8,128)(2,1)S(1)} %bitcast_select_fusion.1.err_ref.refs_2_, bf16[2,256,2304]{2,1,0:T(8,128)(2,1)S(1)} %bitcast_select_fusion.err_ref.refs_3_), custom_call_target="tpu_custom_call" | custom-call | tf_op jit(solution)/shard_map/dec_grad/pallas_call | solution.py:232
  287.0 22.0 %collective-permute-done.14.refs_3_ = bf16[256,2048]{1,0:T(8,128)(2,1)S(1)} collective-permute-done((bf16[256,2048]{1,0:T(8,128)(2,1)S(1)}, bf16[256,2048]{1,0:T(8,128)(2,1)S(1)}, u32[]{:S(2)}, u32[]{:S(2)}) %collective-permute-start.14) | collective-permute-done | bytes 1048608 | tf_op jit(solution)/shard_map/ppermute | solution.py:309
  309.0 8.2 %enc_grad.1 = (f32[1152,2048]{1,0:T(8,128)}, f32[1,2048]{1,0:T(1,128)}) custom-call(s32[1]{0:T(128)} %bitcast.parity_ref, bf16[512,2304]{1,0:T(8,128)(2,1)} %get-tuple-element.24.rows_ref, f32[1,2048]{1,0:T(1,128)S(1)} %copy-done.11, f32[256,2048]{1,0:T(8,128)} %copy-done.5, f32[256,2048]{1,0:T(8,128)} %copy-done.6, ...), custom_call_target="tpu_custom_call" | custom-call | tf_op jit(solution)/shard_map/enc_grad/pallas_call | solution.py:262
  (52 shorter events, 1.4 us)
Async XLA Ops:
  29.8 2.5 copy-start
  30.9 28.6 %copy-start.11 = (f32[1,2048]{1,0:T(1,128)S(1)}, f32[1,2048]{1,0:T(1,128)}, u32[]{:S(2)}) copy-start(f32[1,2048]{1,0:T(1,128)} %bias_in_ref.1) | copy-start | bytes 24580
  30.9 6.0 %collective-permute-start.1 = (bf16[2,2,4,16,2304]{4,3,1,0,2:T(8,128)(2,1)}, bf16[2,2,4,16,2304]{4,3,1,0,2:T(8,128)(2,1)}, u32[]{:S(2)}, u32[]{:S(2)}) collective-permute-start(bf16[2,2,4,16,2304]{4,3,1,0,2:T(8,128)(2,1)} %bitcast.91), channel_id=1, source_target_pairs={{1,9},{8,0},{17,25},{24,16},{3,11},{10,2},{19,27},{26,18},{5,13},{... | collective-permute-start | bytes 3538952 | tf_op jit(solution)/shard_map/ppermute | solution.py:329
  32.3 27.2 %collective-permute-start = (bf16[256,2048]{1,0:T(8,128)(2,1)S(1)}, bf16[256,2048]{1,0:T(8,128)(2,1)S(1)}, u32[]{:S(2)}, u32[]{:S(2)}) collective-permute-start(bf16[256,2048]{1,0:T(8,128)(2,1)S(1)} %copy-done), channel_id=1, source_target_pairs={{0,1},{1,0},{2,3},{3,2},{4,5},{5,4},{6,7},{7,6},{8,9},{9,8},{10,11... | collective-permute-start | bytes 3145736 | tf_op jit(solution)/shard_map/ppermute | solution.py:309
  59.5 11.6 %copy-start.1 = (bf16[256,2048]{1,0:T(8,128)(2,1)S(1)}, bf16[256,2048]{1,0:T(8,128)(2,1)}, u32[]{:S(2)}) copy-start(bf16[256,2048]{1,0:T(8,128)(2,1)} %get-tuple-element.29.own_ref.refs_5_) | copy-start | bytes 3145732
  71.0 3.2 %copy-start.7 = (bf16[256,2048]{1,0:T(8,128)(2,1)}, bf16[256,2048]{1,0:T(8,128)(2,1)S(1)}, u32[]{:S(2)}) copy-start(bf16[256,2048]{1,0:T(8,128)(2,1)S(1)} %get-tuple-element.42.refs_0_) | copy-start | bytes 3145732
  71.0 2.9 collective-permute-start.2
  71.1 25.6 %collective-permute-start.4 = (bf16[256,2048]{1,0:T(8,128)(2,1)S(1)}, bf16[256,2048]{1,0:T(8,128)(2,1)S(1)}, u32[]{:S(2)}, u32[]{:S(2)}) collective-permute-start(bf16[256,2048]{1,0:T(8,128)(2,1)S(1)} %copy-done.1), channel_id=1, source_target_pairs={{0,1},{1,0},{2,3},{3,2},{4,5},{5,4},{6,7},{7,6},{8,9},{9,8},{10,11... | collective-permute-start | bytes 3145736 | tf_op jit(solution)/shard_map/ppermute | solution.py:309
  74.1 1.6 copy-start.13
  75.7 35.6 %copy-start.15 = (f32[4,2304]{1,0:T(4,128)S(1)}, f32[4,2304]{1,0:T(4,128)}, u32[]{:S(2)}) copy-start(f32[4,2304]{1,0:T(4,128)} %param.17) | copy-start | bytes 110596
  96.6 12.3 %copy-start.2 = (bf16[256,2048]{1,0:T(8,128)(2,1)}, bf16[256,2048]{1,0:T(8,128)(2,1)S(1)}, u32[]{:S(2)}) copy-start(bf16[256,2048]{1,0:T(8,128)(2,1)S(1)} %collective-permute-done.4.moved_ref.refs_7_) | copy-start | bytes 3145732
  108.9 1.4 copy-start.4
  110.3 1.0 copy-start.9
  111.3 7.6 %collective-permute-start.5 = (bf16[2,128,2304]{2,1,0:T(8,128)(2,1)}, bf16[2,128,2304]{2,1,0:T(8,128)(2,1)}, u32[]{:S(2)}, u32[]{:S(2)}) collective-permute-start(bf16[2,128,2304]{2,1,0:T(8,128)(2,1)} %get-tuple-element.32), channel_id=1, source_target_pairs={{0,8},{8,0},{16,24},{24,16},{1,9},{9,1},{17,25},{25,17},{2,10},{10... | collective-permute-start | bytes 3538952 | tf_op jit(solution)/shard_map/ppermute | solution.py:312
  111.3 35.3 %all-to-all-start.1 = ((bf16[4,2,2,16,2304]{4,3,2,1,0:T(8,128)(2,1)}), bf16[4,2,2,16,2304]{4,3,2,1,0:T(8,128)(2,1)}, u32[]{:S(2)}, u32[]{:S(2)}) async-start(bf16[4,2,2,16,2304]{4,3,2,1,0:T(8,128)(2,1)} %fusion.5), calls=%async_computation.1 | async-start | bytes 2359296 | tf_op jit(solution)/shard_map/all_to_all | solution.py:315
  117.3 32.2 %collective-permute-start.3 = (bf16[2,64,2304]{2,1,0:T(8,128)(2,1)}, bf16[2,64,2304]{2,1,0:T(8,128)(2,1)}, u32[]{:S(2)}, u32[]{:S(2)}) collective-permute-start(bf16[2,64,2304]{2,1,0:T(8,128)(2,1)} %fusion.6), channel_id=1, source_target_pairs={{0,16},{8,24},{16,0},{24,8},{1,17},{9,25},{17,1},{25,9},{2,18},{10... | collective-permute-start | bytes 1769480 | tf_op jit(solution)/shard_map/ppermute | solution.py:312
  121.1 1.4 copy-start.12
  148.9 9.0 %collective-permute-start.6 = (bf16[2,2,16,2304]{3,2,0,1:T(8,128)(2,1)}, bf16[2,2,16,2304]{3,2,0,1:T(8,128)(2,1)S(1)}, u32[]{:S(2)}, u32[]{:S(2)}) collective-permute-start(bf16[2,2,16,2304]{3,2,0,1:T(8,128)(2,1)} %bitcast.113), channel_id=1, source_target_pairs={{0,1},{1,0},{2,3},{3,2},{4,5},{5,4},{6,7},{7,6},{8,9},{9,8},{10,11... | collective-permute-start | bytes 884744 | tf_op jit(solution)/shard_map/ppermute | solution.py:309
  152.0 22.8 %all-to-all-start = ((bf16[4,2,16,2304]{3,2,1,0:T(8,128)(2,1)}), bf16[4,2,16,2304]{3,2,1,0:T(8,128)(2,1)}, u32[]{:S(2)}, u32[]{:S(2)}) async-start(bf16[4,2,16,2304]{3,2,1,0:T(8,128)(2,1)} %copy.30), calls=%async_computation | async-start | bytes 1179648 | tf_op jit(solution)/shard_map/all_to_all | solution.py:315
  156.3 16.2 %collective-permute-start.10 = (bf16[2,64,2304]{2,1,0:T(8,128)(2,1)}, bf16[2,64,2304]{2,1,0:T(8,128)(2,1)S(1)}, u32[]{:S(2)}, u32[]{:S(2)}) collective-permute-start(bf16[2,64,2304]{2,1,0:T(8,128)(2,1)} %fusion.7), channel_id=1, source_target_pairs={{0,16},{8,24},{16,0},{24,8},{1,17},{9,25},{17,1},{25,9},{2,18},{10... | collective-permute-start | bytes 1769480 | tf_op jit(solution)/shard_map/ppermute | solution.py:312
  158.7 21.8 %collective-permute-start.7 = (bf16[2,16,2304]{2,1,0:T(8,128)(2,1)}, bf16[2,16,2304]{2,1,0:T(8,128)(2,1)}, u32[]{:S(2)}, u32[]{:S(2)}) collective-permute-start(bf16[2,16,2304]{2,1,0:T(8,128)(2,1)} %get-tuple-element.52), channel_id=1, source_target_pairs={{0,16},{8,24},{16,0},{24,8},{1,17},{9,25},{17,1},{25,9},{2,18},{10... | collective-permute-start | bytes 442376 | tf_op jit(solution)/shard_map/ppermute | solution.py:312
  174.7 17.2 %all-to-all-start.3 = ((bf16[4,2,16,2304]{3,2,1,0:T(8,128)(2,1)}), bf16[4,2,16,2304]{3,2,1,0:T(8,128)(2,1)}, u32[]{:S(2)}, u32[]{:S(2)}) async-start(bf16[4,2,16,2304]{3,2,1,0:T(8,128)(2,1)} %copy.35), calls=%async_computation.3 | async-start | bytes 1179648 | tf_op jit(solution)/shard_map/all_to_all | solution.py:315
  211.2 13.9 %collective-permute-start.8 = (bf16[4,2,16,2304]{3,2,1,0:T(8,128)(2,1)}, bf16[4,2,16,2304]{3,2,1,0:T(8,128)(2,1)}, u32[]{:S(2)}, u32[]{:S(2)}) collective-permute-start(bf16[4,2,16,2304]{3,2,1,0:T(8,128)(2,1)} %all_to_all.25), channel_id=1, source_target_pairs={{0,16},{8,24},{16,0},{24,8},{1,17},{9,25},{17,1},{25,9},{2,18},{10... | collective-permute-start | bytes 1769480 | tf_op jit(solution)/shard_map/ppermute | solution.py:312
  213.6 18.6 %all-to-all-start.4 = ((bf16[4,2,16,2304]{3,2,1,0:T(8,128)(2,1)}), bf16[4,2,16,2304]{3,2,1,0:T(8,128)(2,1)}, u32[]{:S(2)}, u32[]{:S(2)}) async-start(bf16[4,2,16,2304]{3,2,1,0:T(8,128)(2,1)} %broadcast_in_dim.85), calls=%async_computation.4 | async-start | bytes 1179648 | tf_op jit(solution)/shard_map/all_to_all | solution.py:315
  227.9 19.8 %collective-permute-start.9 = (bf16[2,4,2,16,2304]{4,3,2,1,0:T(8,128)(2,1)}, bf16[2,4,2,16,2304]{4,3,2,1,0:T(8,128)(2,1)}, u32[]{:S(2)}, u32[]{:S(2)}) collective-permute-start(bf16[2,4,2,16,2304]{4,3,2,1,0:T(8,128)(2,1)} %get-tuple-element.48), channel_id=1, source_target_pairs={{0,8},{8,0},{16,24},{24,16},{1,9},{9,1},{17,25},{25,17},{2,10},{10... | collective-permute-start | bytes 3538952 | tf_op jit(solution)/shard_map/ppermute | solution.py:312
  232.2 15.5 %copy-start.14 = (bf16[1,2,4,2,16,2304]{5,4,3,2,1,0:T(8,128)(2,1)S(1)}, bf16[1,2,4,2,16,2304]{5,4,3,2,1,0:T(8,128)(2,1)}, u32[]{:S(2)}) copy-start(bf16[1,2,4,2,16,2304]{5,4,3,2,1,0:T(8,128)(2,1)} %get-tuple-element.47) | copy-start | bytes 3538948
  232.2 14.2 %collective-permute-start.11 = (bf16[4,2,16,2304]{3,2,1,0:T(8,128)(2,1)}, bf16[4,2,16,2304]{3,2,1,0:T(8,128)(2,1)S(1)}, u32[]{:S(2)}, u32[]{:S(2)}) collective-permute-start(bf16[4,2,16,2304]{3,2,1,0:T(8,128)(2,1)} %all-to-all-done.4), channel_id=1, source_target_pairs={{0,16},{8,24},{16,0},{24,8},{1,17},{9,25},{17,1},{25,9},{2,18},{10... | collective-permute-start | bytes 1769480 | tf_op jit(solution)/shard_map/ppermute | solution.py:312
  247.6 11.5 %collective-permute-start.12 = (bf16[2,4,2,16,2304]{4,3,2,1,0:T(8,128)(2,1)S(1)}, bf16[2,4,2,16,2304]{4,3,2,1,0:T(8,128)(2,1)S(1)}, u32[]{:S(2)}, u32[]{:S(2)}) collective-permute-start(bf16[2,4,2,16,2304]{4,3,2,1,0:T(8,128)(2,1)S(1)} %pad_maximum_fusion.1), channel_id=1, source_target_pairs={{0,8},{8,0},{16,24},{24,16},{1,9},{9,1},{17,25},{25,17},{2,10},{10... | collective-permute-start | bytes 3538952 | tf_op jit(solution)/shard_map/ppermute | solution.py:312
  259.0 1.4 copy-start.5
  260.9 12.8 %copy-start.8 = (bf16[256,2048]{1,0:T(8,128)(2,1)S(1)}, bf16[256,2048]{1,0:T(8,128)(2,1)}, u32[]{:S(2)}) copy-start(bf16[256,2048]{1,0:T(8,128)(2,1)} %copy-done.7) | copy-start | bytes 3145732
  260.9 12.8 %copy-start.10 = (bf16[256,2048]{1,0:T(8,128)(2,1)S(1)}, bf16[256,2048]{1,0:T(8,128)(2,1)}, u32[]{:S(2)}) copy-start(bf16[256,2048]{1,0:T(8,128)(2,1)} %copy-done.9) | copy-start | bytes 3145732
  260.9 26.1 %collective-permute-start.13 = (bf16[256,2048]{1,0:T(8,128)(2,1)S(1)}, bf16[256,2048]{1,0:T(8,128)(2,1)S(1)}, u32[]{:S(2)}, u32[]{:S(2)}) collective-permute-start(bf16[256,2048]{1,0:T(8,128)(2,1)S(1)} %get-tuple-element.38), channel_id=1, source_target_pairs={{0,1},{1,0},{2,3},{3,2},{4,5},{5,4},{6,7},{7,6},{8,9},{9,8},{10,11... | collective-permute-start | bytes 3145736 | tf_op jit(solution)/shard_map/ppermute | solution.py:309
  271.7 1.4 copy-start.6
  273.1 36.0 %collective-permute-start.14 = (bf16[256,2048]{1,0:T(8,128)(2,1)S(1)}, bf16[256,2048]{1,0:T(8,128)(2,1)S(1)}, u32[]{:S(2)}, u32[]{:S(2)}) collective-permute-start(bf16[256,2048]{1,0:T(8,128)(2,1)S(1)} %get-tuple-element.39), channel_id=1, source_target_pairs={{0,1},{1,0},{2,3},{3,2},{4,5},{5,4},{6,7},{7,6},{8,9},{9,8},{10,11... | collective-permute-start | bytes 3145736 | tf_op jit(solution)/shard_map/ppermute | solution.py:309
  273.7 35.3 %copy-start.3 = (bf16[256,2048]{1,0:T(8,128)(2,1)S(1)}, bf16[256,2048]{1,0:T(8,128)(2,1)}, u32[]{:S(2)}) copy-start(bf16[256,2048]{1,0:T(8,128)(2,1)} %copy-done.2) | copy-start | bytes 3145732

commit v2 on v1

--- a/solution.py
+++ b/solution.py
@@ -11,7 +11,7 @@
 CHUNKS = 2
 F32 = jnp.float32
 BF16 = jnp.bfloat16
-LIMITS = pltpu.CompilerParams(vmem_limit_bytes=46 * 2**20)
+LIMITS = pltpu.CompilerParams(vmem_limit_bytes=13 * 2**20)
 
 
 def tile_of(size, limit):
@@ -84,7 +84,9 @@
     )(place, rows, gain, weight)
 
 
-def mlp_body(k_steps, rows_ref, gate_ref, up_ref, down_ref, out_ref, gate_acc, up_acc, hidden):
+def mlp_body(
+    k_steps, rows_ref, gate_ref, up_ref, down_ref, near_ref, far_ref, gate_acc, up_acc, hidden
+):
     step = pl.program_id(0)
 
     @pl.when(step == 0)
@@ -103,7 +105,12 @@
 
     @pl.when(step >= k_steps)
     def _():
-        out_ref[...] = product(hidden[...], down_ref[...], 1, 0).astype(BF16)
+        target = product(hidden[...], down_ref[...], 1, 0).astype(BF16)
+        size = target.shape[0] // (2 * CHUNKS)
+        for c in range(CHUNKS):
+            kept = slice(c * size, (c + 1) * size)
+            near_ref[kept, :] = target[2 * c * size : (2 * c + 1) * size]
+            far_ref[kept, :] = target[(2 * c + 1) * size : (2 * c + 2) * size]
 
 
 def mlp(normed, gate, up, down):
@@ -122,8 +129,8 @@
             pl.BlockSpec((tile, inner), lambda i: (early(i), 0)),
             pl.BlockSpec((inner, tile), lambda i: (0, late(i))),
         ],
-        out_specs=pl.BlockSpec((tokens, tile), lambda i: (0, late(i))),
-        out_shape=jax.ShapeDtypeStruct((tokens, width), BF16),
+        out_specs=[pl.BlockSpec((tokens // 2, tile), lambda i: (0, late(i)))] * 2,
+        out_shape=[jax.ShapeDtypeStruct((tokens // 2, width), BF16)] * 2,
         scratch_shapes=[
             pltpu.VMEM((tokens, inner), F32),
             pltpu.VMEM((tokens, inner), F32),
@@ -133,8 +140,35 @@
     )(normed, gate, up, down)
 
 
+def preload_body(source_ref, out_ref, sem):
+    copy = pltpu.make_async_copy(source_ref, out_ref, sem)
+    copy.start()
+    copy.wait()
+
+
+def preload(decoders):
+    return pl.pallas_call(
+        preload_body,
+        in_specs=[pl.BlockSpec(memory_space=pl.ANY)],
+        out_specs=pl.BlockSpec(memory_space=pltpu.VMEM),
+        out_shape=pltpu.VMEM(decoders.shape, decoders.dtype),
+        scratch_shapes=[pltpu.SemaphoreType.DMA],
+        compiler_params=LIMITS,
+        name="preload",
+    )(decoders)
+
+
 def decode_body(
-    flags_ref, own_ref, moved_ref, bias_ref, weight_ref, target_ref, act_ref, keep_ref, send_ref
+    flags_ref,
+    own_ref,
+    moved_ref,
+    bias_ref,
+    weight_ref,
+    near_ref,
+    far_ref,
+    act_ref,
+    keep_ref,
+    send_ref,
 ):
     slot = pl.program_id(0)
     slots = pl.num_programs(0)
@@ -146,14 +180,15 @@
 
     live = flags_ref[slot].astype(F32)
     mine = flags_ref[slots + slot].astype(F32)
-    recon = product(act_ref[...], weight_ref[0], 1, 0) * live
-    recon = recon - target_ref[...].astype(F32) * mine
+    tile = near_ref.shape[1]
+    column = pl.multiple_of(pl.program_id(1) * tile, tile)
+    recon = product(act_ref[...], weight_ref[slot, :, pl.ds(column, tile)], 1, 0) * live
     half = recon.shape[0] // 2
-    keep_ref[0] = recon[:half]
-    send_ref[0] = recon[half:].astype(BF16)
-
-
-def decode(flags, own, moved, bias, decoders, target, chunk):
+    keep_ref[0] = recon[:half] - near_ref[...].astype(F32) * mine
+    send_ref[0] = (recon[half:] - far_ref[...].astype(F32) * mine).astype(BF16)
+
+
+def decode(flags, own, moved, bias, decoders, targets, chunk):
     size, feats = own.shape
     slots, _, width = decoders.shape
     tile = tile_of(width, 768)
@@ -168,8 +203,9 @@
                 whole,
                 whole,
                 pl.BlockSpec((1, feats), lambda j, d, flags: (0, 0)),
-                pl.BlockSpec((1, feats, tile), lambda j, d, flags: (j, 0, d)),
-                pl.BlockSpec((size, tile), lambda j, d, flags: (chunk, d)),
+                pl.BlockSpec(memory_space=pltpu.VMEM),
+                pl.BlockSpec((size // 2, tile), lambda j, d, flags: (chunk, d)),
+                pl.BlockSpec((size // 2, tile), lambda j, d, flags: (chunk, d)),
             ],
             out_specs=[whole, part, part],
         ),
@@ -180,39 +216,95 @@
         ],
         compiler_params=LIMITS,
         name="decode",
-    )(flags, own, moved, bias, decoders, target)
-
-
-def back_body(err_ref, weight_ref, part_ref, send_ref):
-    part = product(err_ref[0], weight_ref[0], 1, 1)
-    for j in range(1, err_ref.shape[0]):
-        part = part + product(err_ref[j], weight_ref[j], 1, 1)
+    )(flags, own, moved, bias, decoders, *targets)
+
+
+def spread_body(dest_ref, *refs):
+    count = len(refs) - dest_ref.shape[0]
+    for k, out_ref in enumerate(refs[count:]):
+        total = refs[0][:, dest_ref[k]].astype(F32)
+        for value_ref in refs[1:count]:
+            total = total + value_ref[:, dest_ref[k]].astype(F32)
+        out_ref[...] = total.astype(BF16)
+
+
+def choose_body(dest_ref, yes_ref, no_ref, *out_refs):
+    feat_n = len(out_refs)
+    for k, out_ref in enumerate(out_refs):
+        yes, no = yes_ref[:, dest_ref[k]], no_ref[:, dest_ref[k]]
+        out_ref[...] = jnp.where(dest_ref[feat_n] > 0, yes, no)
+
+
+def spread(body, dest, values, feat_n):
+    rows, width = values[0].shape[-2:]
+    groups = values[-1].shape[0]
+    whole = pl.BlockSpec((groups, feat_n, rows, width), lambda i, dest: (0, 0, 0, 0))
+    piece = pl.BlockSpec((groups, rows, width), lambda i, dest: (0, 0, 0))
+    return pl.pallas_call(
+        body,
+        grid_spec=pltpu.PrefetchScalarGridSpec(
+            num_scalar_prefetch=1,
+            grid=(1,),
+            in_specs=[whole] * len(values),
+            out_specs=[piece] * feat_n,
+        ),
+        out_shape=[jax.ShapeDtypeStruct((groups, rows, width), BF16)] * feat_n,
+        compiler_params=LIMITS,
+    )(dest, *values)
+
+
+def back_body(count, flags_ref, *refs):
+    pieces, weight_ref = refs[:count], refs[count]
+    err_ref, part_ref, send_ref = refs[count + 1 :]
+    slots = err_ref.shape[0]
+
+    @pl.when(pl.program_id(0) == 0)
+    def _():
+        blocks, _, rows, _ = pieces[0].shape
+        for j in range(slots):
+            live = flags_ref[j].astype(BF16)
+            for i, piece_ref in enumerate(pieces):
+                for z in range(blocks):
+                    start = (i * blocks + z) * rows
+                    came = flags_ref[2 * slots + z]
+                    err_ref[j, start : start + rows, :] = piece_ref[came, j] * live
+
+    tile = part_ref.shape[1]
+    kept = pl.ds(pl.multiple_of(pl.program_id(0) * tile, tile), tile)
+    part = product(err_ref[0], weight_ref[0, kept, :], 1, 1)
+    for j in range(1, slots):
+        part = part + product(err_ref[j], weight_ref[j, kept, :], 1, 1)
     part_ref[...] = part
     send_ref[...] = part.astype(BF16)
 
 
-def back_product(errors, decoders):
-    slots, size, width = errors.shape
+def back_product(flags, pieces, decoders):
+    blocks, slots, rows, width = pieces[0].shape
+    size = len(pieces) * blocks * rows
     feats = decoders.shape[1]
     tile = tile_of(feats, 512)
     return pl.pallas_call(
-        back_body,
-        grid=(feats // tile,),
-        in_specs=[
-            pl.BlockSpec((slots, size, width), lambda f: (0, 0, 0)),
-            pl.BlockSpec((slots, tile, width), lambda f: (0, f, 0)),
-        ],
-        out_specs=[
-            pl.BlockSpec((size, tile), lambda f: (0, f)),
-            pl.BlockSpec((size, tile), lambda f: (0, f)),
-        ],
+        functools.partial(back_body, len(pieces)),
+        grid_spec=pltpu.PrefetchScalarGridSpec(
+            num_scalar_prefetch=1,
+            grid=(feats // tile,),
+            in_specs=[pl.BlockSpec((blocks, slots, rows, width), lambda f, flags: (0, 0, 0, 0))]
+            * len(pieces)
+            + [pl.BlockSpec(memory_space=pltpu.VMEM)],
+            out_specs=[
+                pl.BlockSpec((slots, size, width), lambda f, flags: (0, 0, 0)),
+                pl.BlockSpec((size, tile), lambda f, flags: (0, f)),
+                pl.BlockSpec((size, tile), lambda f, flags: (0, f)),
+            ],
+        ),
         out_shape=[
+            jax.ShapeDtypeStruct((slots, size, width), BF16),
             jax.ShapeDtypeStruct((size, feats), F32),
             jax.ShapeDtypeStruct((size, feats), BF16),
         ],
         compiler_params=LIMITS,
         name="back_product",
-    )(errors, decoders)
+    )(flags, *pieces, decoders)
 
 
 def dec_grad_body(*refs):
@@ -299,6 +391,7 @@
     outer = layers // 2
     source = lax.axis_index("layer")
     parity = lax.axis_index("par")
+    place_z = lax.axis_index("feat")
     slots = dec_weight.shape[2]
     _, tokens, width = residual.shape
     half_width = enc_weight.shape[1]
@@ -311,8 +404,8 @@
     def over_layer(value, mask):
         return lax.ppermute(value, "layer", [(s, s ^ mask) for s in range(layers)])
 
-    def over_feat(value):
-        return lax.all_to_all(value, "feat", 0, 0, tiled=True)
+    def over_feat(value, shift):
+        return lax.ppermute(value, "feat", [(z, (z + shift) % feat_n) for z in range(feat_n)])
 
     index = jnp.arange(CHUNKS * layers, dtype=jnp.int32)
     table = index ^ (source % 2 * outer + source // 2)
@@ -322,79 +415,93 @@
     pre_moved = []
     for c in range(CHUNKS):
         pre_moved.append(over_par(pre_send[c]))
-    target_part = mlp(normed, gate_weight[0], up_weight[0], down_weight[0])
+    targets = mlp(normed, gate_weight[0], up_weight[0], down_weight[0])
 
     pairs = [(s * 2 + 1 - s % 2, (s ^ 1) * 2 + 1 - s % 2) for s in range(layers)]
-    halves = target_part.reshape(CHUNKS, 2, outer, feat_n, rows_n, width)
-    handed = lax.ppermute(halves[:, 1], ("layer", "par"), pairs)
-    moving = jnp.where(source % 2 == parity, handed, halves[:, 0])
-    moving = moving.transpose(2, 0, 1, 3, 4)
-    target_moved = over_feat(moving)
+    handed = lax.ppermute(targets[1], ("layer", "par"), pairs)
 
     slot_ids = jnp.arange(slots, dtype=jnp.int32)
-    decoders = dec_weight[0, 0]
+    feat_ids = jnp.arange(feat_n, dtype=jnp.int32)
+    outer_ids = jnp.arange(outer, dtype=jnp.int32)
     live = 2 * slot_ids + parity >= source
     mine = (slot_ids == source // 2) & (source % 2 == parity)
-    flags = jnp.concatenate([live, mine]).astype(jnp.int32)
-    bias_rows = lax.dynamic_index_in_dim(
-        dec_bias.reshape(slots, 2, width), parity, 1, keepdims=False
+    came = (feat_ids - place_z) % feat_n
+    flags = jnp.concatenate([live.astype(jnp.int32), mine.astype(jnp.int32), came])
+    own_target = jnp.full((1,), source % 2 == parity, jnp.int32)
+    dest = jnp.concatenate([(feat_ids + place_z) % feat_n, own_target])
+    chosen = (slot_ids[None] == (outer_ids[:, None] ^ (source // 2))).astype(F32)
+    bias_rows = jnp.stack(
+        [
+            lax.dynamic_index_in_dim(dec_bias, 2 * j + parity, 0, keepdims=False)
+            for j in range(slots)
+        ]
     )
+    flags, dest, chosen, bias_rows, decoders, _ = lax.optimization_barrier(
+        (flags, dest, chosen, bias_rows, dec_weight, targets[0])
+    )
+    decoders = preload(decoders[0, 0])
 
     actives = []
-    wholes = []
-    last = moving
+    spreads = []
     for c in range(CHUNKS):
-        active, keep, send = decode(
-            flags, pre_send[c], tied(pre_moved[c], last), enc_bias, decoders, target_part, c
-        )
+        seen = pre_moved[c]
+        if c:
+            seen = tied(seen, leaving)
+        active, keep, send = decode(flags, pre_send[c], seen, enc_bias, decoders, targets, c)
         actives.append(active)
         got = over_layer(send, 1)
-        both = (keep + got.astype(F32)).reshape(slots, outer, feat_n * rows_n, width)
-        whole = both[:, 0]
+        keep = keep.reshape(slots, outer * feat_n, rows_n, width)
+        got = got.reshape(keep.shape)
+        arrived = [keep, got]
+        leaving = got
         for high in range(1, outer):
-            last = both[:, high].astype(BF16)
-            got = over_layer(last, 2 * high)
-            whole = whole + got.astype(F32)
-        wholes.append(whole.astype(BF16).reshape(slots, feat_n, rows_n, width).swapaxes(0, 1))
-
-    summed = jnp.sum(tied(target_moved, last).astype(F32), axis=0)
-    crossed = over_par(summed.astype(BF16).transpose(1, 0, 2, 3))
+            there = slice(high * feat_n, (high + 1) * feat_n)
+            leaving = (keep[:, there] + got[:, there].astype(F32)).astype(BF16)
+            arrived.append(over_layer(leaving, 2 * high))
+        spreads.append(spread(spread_body, dest[:feat_n], arrived, feat_n))
+        if c == 0:
+            chunks = (CHUNKS * outer, feat_n, rows_n, width)
+            pair = (tied(handed, leaving).reshape(chunks), targets[0].reshape(chunks))
+            moving = spread(choose_body, dest, pair, feat_n)
+            target_moved = [over_feat(moving[k], k) for k in range(1, feat_n)]
+
+    summed = moving[0].astype(F32)
+    for part in target_moved:
+        summed = summed + part.astype(F32)
+    summed = summed.astype(BF16).reshape(CHUNKS, outer, rows_n, width)
     far_target = 0.0
     for high in range(outer):
-        got = crossed[0] if high == 0 else over_layer(crossed[high], 2 * high)
-        chosen = slot_ids == ((source // 2) ^ high)
-        far_target = far_target + jnp.where(
-            chosen[:, None, None, None], got[None].astype(F32), 0.0
-        )
+        got = over_par(summed[:, high])
+        if high:
+            got = over_layer(got, 2 * high)
+        far_target = far_target + chosen[high][:, None, None, None] * got[None].astype(F32)
 
     gathered = []
     for c in range(CHUNKS):
-        got = over_feat(wholes[c])
+        came = [over_feat(spreads[c][k], k) for k in range(1, feat_n)]
         if c:
-            got = tied(got, error)
-        total = jnp.sum(got.astype(F32), axis=0)
+            came[0] = tied(came[0], error)
+        total = spreads[c][0].astype(F32)
+        for part in came:
+            total = total + part.astype(F32)
         error = (total - far_target[:, c] + bias_rows[:, None]) * 0.0625
         error = error.astype(BF16)
-        gathered.append(over_feat(jnp.broadcast_to(error[None], (feat_n,) + error.shape)))
+        came = [over_feat(error, feat_n - k) for k in range(1, feat_n)]
+        gathered.append(jnp.stack([error] + came))
 
     errors = []
     parts = []
     moved = []
     for c in range(CHUNKS):
-        rows = [gathered[c]]
+        pieces = [gathered[c]]
         for high in range(1, outer):
-            rows.append(over_layer(gathered[c], 2 * high))
-        rows = jnp.stack(rows)
-        other = over_layer(rows, 1)
-        if c:
-            rows, other = lax.optimization_barrier((rows, other, parts[-1]))[:2]
-        rows = jnp.stack([rows, other])
-        rows = rows.transpose(3, 0, 1, 2, 4, 5).reshape(slots, size, width)
-        errors.append(jnp.where(live[:, None, None], rows, jnp.zeros_like(rows)))
-        part, send = back_product(errors[c], decoders)
+            pieces.append(over_layer(gathered[c], 2 * high))
+        pieces = pieces + [over_layer(piece, 1) for piece in pieces]
+        error, part, send = back_product(flags, pieces, decoders)
+        errors.append(error)
         parts.append(part)
         moved.append(over_par(send))
-    dec_grad = dec_grad_product(actives, errors[:-1] + [tied(errors[-1], send)])
+    dec_grad = dec_grad_product(actives, errors)
     enc_grad, bias_grad = enc_grad_product(
         parity_arg, normed, half_width, enc_bias, parts, moved, pre_send, pre_moved
     )

time: 318 us -> 233 us (0.73)
  the two profiles are of different devices: /device:TPU:0 before, /device:TPU:10 now
where the time goes in v2:
time: 233 us
  waiting for transfers between devices  112 us (48%)
  Pallas kernels  77.7 us (33%)
  starting transfers between devices  33.7 us (14%)
  local copies, waits for them, and re-layouts  6.97 us (3%)
    ppermute x6, waiting for transfers between devices, over_par(): return lax.ppermute(value, 'par', [(0, 1), (1, 0)])  49.8 us
    ppermute x11, waiting for transfers between devices, over_layer(): return lax.ppermute(value, 'layer', [(s, s ^ mask) for s in range(layers)])  33.4 us
    ppermute x15, waiting for transfers between devices, over_feat(): lax.ppermute(value, 'feat', [(z, (z + shift) % feat_n) for z in range(fea...  27.3 us
    ppermute x15, starting transfers between devices, over_feat(): lax.ppermute(value, 'feat', [(z, (z + shift) % feat_n) for z in range(fea...  20.7 us
    pallas_call x1, Pallas kernels, mlp(): pl.pallas_call(functools.partial(mlp_body, steps), grid=(2 * steps,), in_...  15.5 us
    pallas_call x2, Pallas kernels, decode(): pl.pallas_call(decode_body, grid_spec=pltpu.PrefetchScalarGridSpec(num_sc...  15.3 us
    pallas_call x2, Pallas kernels, back_product(): pl.pallas_call(functools.partial(back_body, len(pieces)), grid_spec=pltpu...  13.2 us
    pallas_call x1, Pallas kernels, dec_grad_product(): pl.pallas_call(dec_grad_body, grid=(feats // tile,), in_specs=[pl.BlockSp...  13.2 us
  transfers between devices with their start and end apart: 33, of which 18 were waited for; matrix products, arithmetic and copies ran while one was open for 1% of the time, Pallas kernels for 23%

profile of v2, /device:TPU:10, one launch (start us, length us, event | category | flops | bytes accessed | tf_op | source)
XLA Modules:
  0.0 232.6 jit_solution(14266201405239736200)
XLA Ops:
  0.7 0.6 pad_add_fusion.place_ref
  1.3 10.2 %encode.1 = (bf16[512,2304]{1,0:T(8,128)(2,1)}, bf16[256,2048]{1,0:T(8,128)(2,1)}, bf16[256,2048]{1,0:T(8,128)(2,1)}) custom-call(s32[9]{0:T(128)} %pad_add_fusion.place_ref, bf16[512,2304]{1,0:T(8,128)(2,1)} %bitcast.76, f32[1,2304]{1,0:T(1,128)} %gain_ref.1, f32[1152,2048]{1,0:T(8,128)} %bitcast.72), custom_call_target="tpu_custom_call" | custom-call | tf_op jit(solution)/shard_map/encode/pallas_call | solution.py:67
  11.5 1.5 collective-permute-start
  13.1 15.5 %mlp.1 = (bf16[256,2304]{1,0:T(8,128)(2,1)}, bf16[256,2304]{1,0:T(8,128)(2,1)}) custom-call(bf16[512,2304]{1,0:T(8,128)(2,1)} %get-tuple-element.42.rows_ref, bf16[2304,1152]{1,0:T(8,128)(2,1)} %bitcast.73, bf16[2304,1152]{1,0:T(8,128)(2,1)} %bitcast.74, bf16[1152,2304]{1,0:T(8,128)(2,1)} %bitcast.75), custom_call_target="tpu_custom_call" | custom-call | tf_op jit(solution)/shard_map/mlp/pallas_call | solution.py:123
  28.8 6.4 %copy-done = bf16[1,1,2,2048,2304]{4,3,2,1,0:T(8,128)(2,1)S(1)} copy-done((bf16[1,1,2,2048,2304]{4,3,2,1,0:T(8,128)(2,1)S(1)}, bf16[1,1,2,2048,2304]{4,3,2,1,0:T(8,128)(2,1)}, u32[]{:S(2)}) %copy-start) | copy-done | bytes 18874392
  35.2 1.3 preload.1.weight_ref.refs_4_
  36.6 0.2 copy-done.3
  36.8 0.3 copy-done.4
  37.1 7.7 %decode.2 = (bf16[256,2048]{1,0:T(8,128)(2,1)S(1)}, f32[2,128,2304]{2,1,0:T(8,128)S(1)}, bf16[2,128,2304]{2,1,0:T(8,128)(2,1)S(1)}) custom-call(s32[8]{0:T(128)S(1)} %pad_add_fusion.1.flags_ref, bf16[256,2048]{1,0:T(8,128)(2,1)S(1)} %copy-done.4, bf16[256,2048]{1,0:T(8,128)(2,1)S(1)} %collective-permute-done.moved_ref.refs_6_, f32[1,2048]{1,0:T(1,128)S(1)} %copy-done.6, ...), custom_call_target="tpu_custom_call" | custom-call | tf_op jit(solution)/shard_map/decode/pallas_call | solution.py:197
  44.9 1.3 collective-permute-start.6
  46.2 2.2 collective-permute-start.19
  48.6 1.1 collective-permute-done.6
  49.6 0.7 shard_map.113
  50.3 1.6 collective-permute-start.7
  51.9 1.2 collective-permute-start.8
  53.2 1.8 collective-permute-start.9
  55.0 0.5 collective-permute-start.2
  55.5 16.9 %collective-permute-done.19.moved_ref.refs_7_ = bf16[256,2048]{1,0:T(8,128)(2,1)S(1)} collective-permute-done((bf16[256,2048]{1,0:T(8,128)(2,1)S(1)}, bf16[256,2048]{1,0:T(8,128)(2,1)S(1)}, u32[]{:S(2)}, u32[]{:S(2)}) %collective-permute-start.19) | collective-permute-done | bytes 1048608 | tf_op jit(solution)/shard_map/ppermute | solution.py:402
  72.4 7.7 %decode.3 = (bf16[256,2048]{1,0:T(8,128)(2,1)S(1)}, f32[2,128,2304]{2,1,0:T(8,128)S(1)}, bf16[2,128,2304]{2,1,0:T(8,128)(2,1)S(1)}) custom-call(s32[8]{0:T(128)S(1)} %pad_add_fusion.1.flags_ref, bf16[256,2048]{1,0:T(8,128)(2,1)S(1)} %copy-done.5, bf16[256,2048]{1,0:T(8,128)(2,1)S(1)} %collective-permute-done.19.moved_ref.refs_7_, f32[1,2048]{1,0:T(1,128)S(1)} %copy-done.6, ...), custom_call_target="tpu_custom_call" | custom-call | tf_op jit(solution)/shard_map/decode/pallas_call | solution.py:197
  80.0 0.2 collective-permute-start.20
  80.2 0.2 add_convert_fusion
  80.4 0.4 collective-permute-start.11
  80.9 1.7 collective-permute-start.10
  82.5 4.7 %collective-permute-done.11 = bf16[2,16,2304]{2,1,0:T(8,128)(2,1)S(1)} collective-permute-done((bf16[2,16,2304]{2,1,0:T(8,128)(2,1)S(1)}, bf16[2,16,2304]{2,1,0:T(8,128)(2,1)S(1)}, u32[]{:S(2)}, u32[]{:S(2)}) %collective-permute-start.11) | collective-permute-done | bytes 147488 | tf_op jit(solution)/shard_map/ppermute | solution.py:402
  87.2 0.5 collective-permute-start.12
  87.8 2.1 collective-permute-done.10
  89.8 0.9 shard_map.112
  90.8 1.6 collective-permute-start.3
  92.4 1.2 collective-permute-start.4
  93.6 1.8 collective-permute-start.5
  95.6 0.6 collective-permute-start.21
  96.2 0.1 multiply_add_fusion
  96.3 13.2 %collective-permute-done.21.refs_2_ = bf16[2,4,16,2304]{3,2,1,0:T(8,128)(2,1)S(1)} collective-permute-done((bf16[2,4,16,2304]{3,2,1,0:T(8,128)(2,1)S(1)}, bf16[2,4,16,2304]{3,2,1,0:T(8,128)(2,1)S(1)}, u32[]{:S(2)}, u32[]{:S(2)}) %collective-permute-start.21) | collective-permute-done | bytes 589856 | tf_op jit(solution)/shard_map/ppermute | solution.py:405
  109.6 0.9 shard_map.114
  110.5 0.4 collective-permute-start.22
  110.9 3.3 %collective-permute-start.23 = (bf16[2,16,2304]{2,1,0:T(8,128)(2,1)S(1)}, bf16[2,16,2304]{2,1,0:T(8,128)(2,1)S(1)}, u32[]{:S(2)}, u32[]{:S(2)}) collective-permute-start(bf16[2,16,2304]{2,1,0:T(8,128)(2,1)S(1)} %get-tuple-element.70), channel_id=1, source_target_pairs={{0,4},{2,6},{4,0},{6,2},{1,5},{3,7},{5,1},{7,3},{8,12},{10,14},{12... | collective-permute-start | bytes 442376 | tf_op jit(solution)/shard_map/ppermute | solution.py:408
  114.2 0.1 fusion.9
  114.3 2.1 collective-permute-start.15
  116.4 1.8 collective-permute-start.14
  118.2 1.1 collective-permute-done.22
  119.3 1.1 collective-permute-start.13
  120.4 10.1 %collective-permute-done.23 = bf16[2,16,2304]{2,1,0:T(8,128)(2,1)S(1)} collective-permute-done((bf16[2,16,2304]{2,1,0:T(8,128)(2,1)S(1)}, bf16[2,16,2304]{2,1,0:T(8,128)(2,1)S(1)}, u32[]{:S(2)}, u32[]{:S(2)}) %collective-permute-start.23) | collective-permute-done | bytes 147488 | tf_op jit(solution)/shard_map/ppermute | solution.py:408
  130.5 2.7 %collective-permute-done.24 = bf16[2,16,2304]{2,1,0:T(8,128)(2,1)S(1)} collective-permute-done((bf16[2,16,2304]{2,1,0:T(8,128)(2,1)S(1)}, bf16[2,16,2304]{2,1,0:T(8,128)(2,1)S(1)}, u32[]{:S(2)}, u32[]{:S(2)}) %collective-permute-start.24) | collective-permute-done | bytes 147488 | tf_op jit(solution)/shard_map/ppermute | solution.py:408
  133.2 0.1 fusion.5
  133.4 0.7 collective-permute-start.26
  134.1 1.9 collective-permute-start.25
  136.1 1.6 collective-permute-done.14
  137.7 6.6 %collective-permute-done.13 = bf16[2,16,2304]{2,1,0:T(8,128)(2,1)S(1)} collective-permute-done((bf16[2,16,2304]{2,1,0:T(8,128)(2,1)S(1)}, bf16[2,16,2304]{2,1,0:T(8,128)(2,1)S(1)}, u32[]{:S(2)}, u32[]{:S(2)}) %collective-permute-start.13) | collective-permute-done | bytes 147488 | tf_op jit(solution)/shard_map/ppermute | solution.py:408
  144.3 0.6 collective-permute-start.16
  144.9 1.4 collective-permute-done.27
  146.3 1.6 collective-permute-done.26
  147.9 2.2 collective-permute-done.25
  150.2 0.6 collective-permute-start.28
  150.8 9.8 %collective-permute-done.16.refs_1_ = bf16[4,2,16,2304]{3,2,1,0:T(8,128)(2,1)S(1)} collective-permute-done((bf16[4,2,16,2304]{3,2,1,0:T(8,128)(2,1)S(1)}, bf16[4,2,16,2304]{3,2,1,0:T(8,128)(2,1)S(1)}, u32[]{:S(2)}, u32[]{:S(2)}) %collective-permute-start.16) | collective-permute-done | bytes 589856 | tf_op jit(solution)/shard_map/ppermute | solution.py:405
  160.6 0.5 collective-permute-start.29
  161.1 10.3 %collective-permute-done.28.refs_1_ = bf16[4,2,16,2304]{3,2,1,0:T(8,128)(2,1)S(1)} collective-permute-done((bf16[4,2,16,2304]{3,2,1,0:T(8,128)(2,1)S(1)}, bf16[4,2,16,2304]{3,2,1,0:T(8,128)(2,1)S(1)}, u32[]{:S(2)}, u32[]{:S(2)}) %collective-permute-start.28) | collective-permute-done | bytes 589856 | tf_op jit(solution)/shard_map/ppermute | solution.py:405
  171.5 6.6 %back_product.2 = (bf16[2,256,2304]{2,1,0:T(8,128)(2,1)S(1)}, f32[256,2048]{1,0:T(8,128)S(1)}, bf16[256,2048]{1,0:T(8,128)(2,1)S(1)}) custom-call(s32[8]{0:T(128)S(1)} %pad_add_fusion.1.flags_ref, bf16[4,2,16,2304]{3,2,1,0:T(8,128)(2,1)S(1)} %pad_maximum_fusion.refs_0_, bf16[4,2,16,2304]{3,2,1,0:T(8,128)(2,1)S(1)} %collective-permute-done.16.refs_1_, ...), custom_call_target="tpu_custom_call" | custom-call | tf_op jit(solution)/shard_map/back_product/pallas_call | solution.py:286
  178.1 0.5 collective-permute-start.31
  178.7 6.6 %back_product.3 = (bf16[2,256,2304]{2,1,0:T(8,128)(2,1)S(1)}, f32[256,2048]{1,0:T(8,128)S(1)}, bf16[256,2048]{1,0:T(8,128)(2,1)S(1)}) custom-call(s32[8]{0:T(128)S(1)} %pad_add_fusion.1.flags_ref, bf16[4,2,16,2304]{3,2,1,0:T(8,128)(2,1)S(1)} %pad_maximum_fusion.1.refs_0_, bf16[4,2,16,2304]{3,2,1,0:T(8,128)(2,1)S(1)} %collective-permute-done.28.refs_1_, ...), custom_call_target="tpu_custom_call" | custom-call | tf_op jit(solution)/shard_map/back_product/pallas_call | solution.py:286
  185.3 1.6 collective-permute-start.32
  186.9 13.2 %dec_grad.1 = bf16[2,2048,2304]{2,1,0:T(8,128)(2,1)} custom-call(bf16[256,2048]{1,0:T(8,128)(2,1)S(1)} %get-tuple-element.77.refs_0_, bf16[256,2048]{1,0:T(8,128)(2,1)S(1)} %get-tuple-element.78.refs_1_, bf16[2,256,2304]{2,1,0:T(8,128)(2,1)S(1)} %get-tuple-element.79.refs_2_, bf16[2,256,2304]{2,1,0:T(8,128)(2,1)S(1)} %get-tuple-element.80.refs_3_), custom_call_target="tpu_custom_call" | custom-call | tf_op jit(solution)/shard_map/dec_grad/pallas_call | solution.py:324
  200.1 4.1 %collective-permute-done.31.refs_2_ = bf16[256,2048]{1,0:T(8,128)(2,1)S(1)} collective-permute-done((bf16[256,2048]{1,0:T(8,128)(2,1)S(1)}, bf16[256,2048]{1,0:T(8,128)(2,1)S(1)}, u32[]{:S(2)}, u32[]{:S(2)}) %collective-permute-start.31) | collective-permute-done | bytes 1048608 | tf_op jit(solution)/shard_map/ppermute | solution.py:402
  204.2 22.0 %collective-permute-done.32.refs_3_ = bf16[256,2048]{1,0:T(8,128)(2,1)S(1)} collective-permute-done((bf16[256,2048]{1,0:T(8,128)(2,1)S(1)}, bf16[256,2048]{1,0:T(8,128)(2,1)S(1)}, u32[]{:S(2)}, u32[]{:S(2)}) %collective-permute-start.32) | collective-permute-done | bytes 1048608 | tf_op jit(solution)/shard_map/ppermute | solution.py:402
  226.2 6.4 %enc_grad.1 = (f32[1152,2048]{1,0:T(8,128)}, f32[1,2048]{1,0:T(1,128)}) custom-call(s32[1]{0:T(128)} %bitcast.parity_ref, bf16[512,2304]{1,0:T(8,128)(2,1)S(1)} %copy-done.2, f32[1,2048]{1,0:T(1,128)S(1)} %copy-done.6, f32[256,2048]{1,0:T(8,128)S(1)} %get-tuple-element.62.refs_0_, f32[256,2048]{1,0:T(8,128)S(1)} %get-tuple-element.72.refs_1_, ...), custom_call_target="tpu_custom_call" | custom-call | tf_op jit(solution)/shard_map/enc_grad/pallas_call | solution.py:354
  (52 shorter events, 1.0 us)
Async XLA Ops:
  11.5 25.1 %collective-permute-start = (bf16[256,2048]{1,0:T(8,128)(2,1)}, bf16[256,2048]{1,0:T(8,128)(2,1)S(1)}, u32[]{:S(2)}, u32[]{:S(2)}) collective-permute-start(bf16[256,2048]{1,0:T(8,128)(2,1)} %get-tuple-element.46.own_ref.refs_4_), channel_id=1, source_target_pairs={{0,1},{1,0},{2,3},{3,2},{4,5},{5,4},{6,7},{7,6},{8,9},{9,8},{10,11... | collective-permute-start | bytes 3145736 | tf_op jit(solution)/shard_map/ppermute | solution.py:402
  13.1 15.7 %copy-start.7 = (f32[4,2304]{1,0:T(4,128)S(1)}, f32[4,2304]{1,0:T(4,128)}, u32[]{:S(2)}) copy-start(f32[4,2304]{1,0:T(4,128)} %param.17) | copy-start | bytes 110596
  28.8 6.4 %copy-start = (bf16[1,1,2,2048,2304]{4,3,2,1,0:T(8,128)(2,1)S(1)}, bf16[1,1,2,2048,2304]{4,3,2,1,0:T(8,128)(2,1)}, u32[]{:S(2)}) copy-start(bf16[1,1,2,2048,2304]{4,3,2,1,0:T(8,128)(2,1)} %param.16) | copy-start | bytes 56623108
  35.2 1.4 copy-start.1
  35.2 1.6 copy-start.3
  35.2 1.9 copy-start.4
  35.2 1.9 copy-start.6
  37.1 9.1 %copy-start.5 = (bf16[256,2048]{1,0:T(8,128)(2,1)S(1)}, bf16[256,2048]{1,0:T(8,128)(2,1)}, u32[]{:S(2)}) copy-start(bf16[256,2048]{1,0:T(8,128)(2,1)} %get-tuple-element.63.own_ref.refs_5_) | copy-start | bytes 3145732
  44.8 3.6 %collective-permute-start.1 = (bf16[2,128,2304]{2,1,0:T(8,128)(2,1)S(1)}, bf16[2,128,2304]{2,1,0:T(8,128)(2,1)S(1)}, u32[]{:S(2)}, u32[]{:S(2)}) collective-permute-start(bf16[2,128,2304]{2,1,0:T(8,128)(2,1)S(1)} %get-tuple-element.50), channel_id=1, source_target_pairs={{0,8},{8,0},{16,24},{24,16},{1,9},{9,1},{17,25},{25,17},{2,10},{10... | collective-permute-start | bytes 3538952 | tf_op jit(solution)/shard_map/ppermute | solution.py:405
  44.9 4.7 %collective-permute-start.6 = (bf16[256,2304]{1,0:T(8,128)(2,1)S(1)}, bf16[256,2304]{1,0:T(8,128)(2,1)S(1)}, u32[]{:S(2)}, u32[]{:S(2)}) collective-permute-start(bf16[256,2304]{1,0:T(8,128)(2,1)S(1)} %copy-done.3), channel_id=1, source_target_pairs={{1,9},{8,0},{17,25},{24,16},{3,11},{10,2},{19,27},{26,18},{5,13},{... | collective-permute-start | bytes 3538952 | tf_op jit(solution)/shard_map/ppermute | solution.py:421
  46.2 26.2 %collective-permute-start.19 = (bf16[256,2048]{1,0:T(8,128)(2,1)S(1)}, bf16[256,2048]{1,0:T(8,128)(2,1)S(1)}, u32[]{:S(2)}, u32[]{:S(2)}) collective-permute-start(bf16[256,2048]{1,0:T(8,128)(2,1)S(1)} %copy-done.5), channel_id=1, source_target_pairs={{0,1},{1,0},{2,3},{3,2},{4,5},{5,4},{6,7},{7,6},{8,9},{9,8},{10,11... | collective-permute-start | bytes 3145736 | tf_op jit(solution)/shard_map/ppermute | solution.py:402
  50.3 29.9 %collective-permute-start.7 = (bf16[4,16,2304]{2,1,0:T(8,128)(2,1)S(1)}, bf16[4,16,2304]{2,1,0:T(8,128)(2,1)S(1)}, u32[]{:S(2)}, u32[]{:S(2)}) collective-permute-start(bf16[4,16,2304]{2,1,0:T(8,128)(2,1)S(1)} %get-tuple-element.58), channel_id=1, source_target_pairs={{0,2},{2,4},{4,6},{6,0},{1,3},{3,5},{5,7},{7,1},{8,10},{10,12},{12... | collective-permute-start | bytes 884744 | tf_op jit(solution)/shard_map/ppermute | solution.py:408
  51.9 28.3 %collective-permute-start.8 = (bf16[4,16,2304]{2,1,0:T(8,128)(2,1)S(1)}, bf16[4,16,2304]{2,1,0:T(8,128)(2,1)S(1)}, u32[]{:S(2)}, u32[]{:S(2)}) collective-permute-start(bf16[4,16,2304]{2,1,0:T(8,128)(2,1)S(1)} %get-tuple-element.59), channel_id=1, source_target_pairs={{0,4},{2,6},{4,0},{6,2},{1,5},{3,7},{5,1},{7,3},{8,12},{10,14},{12... | collective-permute-start | bytes 884744 | tf_op jit(solution)/shard_map/ppermute | solution.py:408
  53.2 27.1 %collective-permute-start.9 = (bf16[4,16,2304]{2,1,0:T(8,128)(2,1)S(1)}, bf16[4,16,2304]{2,1,0:T(8,128)(2,1)S(1)}, u32[]{:S(2)}, u32[]{:S(2)}) collective-permute-start(bf16[4,16,2304]{2,1,0:T(8,128)(2,1)S(1)} %get-tuple-element.60), channel_id=1, source_target_pairs={{0,6},{2,0},{4,2},{6,4},{1,7},{3,1},{5,3},{7,5},{8,14},{10,8},{12,... | collective-permute-start | bytes 884744 | tf_op jit(solution)/shard_map/ppermute | solution.py:408
  55.0 34.9 %collective-permute-start.2 = (bf16[2,4,16,2304]{3,2,1,0:T(8,128)(2,1)S(1)}, bf16[2,4,16,2304]{3,2,1,0:T(8,128)(2,1)S(1)}, u32[]{:S(2)}, u32[]{:S(2)}) collective-permute-start(bf16[2,4,16,2304]{3,2,1,0:T(8,128)(2,1)S(1)} %fusion.1), channel_id=1, source_target_pairs={{0,16},{8,24},{16,0},{24,8},{1,17},{9,25},{17,1},{25,9},{2,18},{10... | collective-permute-start | bytes 1769480 | tf_op jit(solution)/shard_map/ppermute | solution.py:405
  80.0 15.4 %collective-permute-start.20 = (bf16[2,128,2304]{2,1,0:T(8,128)(2,1)S(1)}, bf16[2,128,2304]{2,1,0:T(8,128)(2,1)S(1)}, u32[]{:S(2)}, u32[]{:S(2)}) collective-permute-start(bf16[2,128,2304]{2,1,0:T(8,128)(2,1)S(1)} %get-tuple-element.66), channel_id=1, source_target_pairs={{0,8},{8,0},{16,24},{24,16},{1,9},{9,1},{17,25},{25,17},{2,10},{10... | collective-permute-start | bytes 3538952 | tf_op jit(solution)/shard_map/ppermute | solution.py:405
  80.4 6.8 %collective-permute-start.11 = (bf16[2,16,2304]{2,1,0:T(8,128)(2,1)S(1)}, bf16[2,16,2304]{2,1,0:T(8,128)(2,1)S(1)}, u32[]{:S(2)}, u32[]{:S(2)}) collective-permute-start(bf16[2,16,2304]{2,1,0:T(8,128)(2,1)S(1)} %get-tuple-element.82), channel_id=1, source_target_pairs={{0,1},{1,0},{2,3},{3,2},{4,5},{5,4},{6,7},{7,6},{8,9},{9,8},{10,11... | collective-permute-start | bytes 442376 | tf_op jit(solution)/shard_map/ppermute | solution.py:402
  80.9 8.9 %collective-permute-start.10 = (bf16[2,16,2304]{2,1,0:T(8,128)(2,1)S(1)}, bf16[2,16,2304]{2,1,0:T(8,128)(2,1)S(1)}, u32[]{:S(2)}, u32[]{:S(2)}) collective-permute-start(bf16[2,16,2304]{2,1,0:T(8,128)(2,1)S(1)} %get-tuple-element.81), channel_id=1, source_target_pairs={{0,1},{1,0},{2,3},{3,2},{4,5},{5,4},{6,7},{7,6},{8,9},{9,8},{10,11... | collective-permute-start | bytes 442376 | tf_op jit(solution)/shard_map/ppermute | solution.py:402
  87.2 8.2 %collective-permute-start.12 = (bf16[2,16,2304]{2,1,0:T(8,128)(2,1)S(1)}, bf16[2,16,2304]{2,1,0:T(8,128)(2,1)S(1)}, u32[]{:S(2)}, u32[]{:S(2)}) collective-permute-start(bf16[2,16,2304]{2,1,0:T(8,128)(2,1)S(1)} %collective-permute-done.11), channel_id=1, source_target_pairs={{0,16},{8,24},{16,0},{24,8},{1,17},{9,25},{17,1},{25,9},{2,18},{10... | collective-permute-start | bytes 442376 | tf_op jit(solution)/shard_map/ppermute | solution.py:405
  90.8 23.4 %collective-permute-start.3 = (bf16[2,16,2304]{2,1,0:T(8,128)(2,1)S(1)}, bf16[2,16,2304]{2,1,0:T(8,128)(2,1)S(1)}, u32[]{:S(2)}, u32[]{:S(2)}) collective-permute-start(bf16[2,16,2304]{2,1,0:T(8,128)(2,1)S(1)} %get-tuple-element.52), channel_id=1, source_target_pairs={{0,2},{2,4},{4,6},{6,0},{1,3},{3,5},{5,7},{7,1},{8,10},{10,12},{12... | collective-permute-start | bytes 442376 | tf_op jit(solution)/shard_map/ppermute | solution.py:408
  92.4 21.8 %collective-permute-start.4 = (bf16[2,16,2304]{2,1,0:T(8,128)(2,1)S(1)}, bf16[2,16,2304]{2,1,0:T(8,128)(2,1)S(1)}, u32[]{:S(2)}, u32[]{:S(2)}) collective-permute-start(bf16[2,16,2304]{2,1,0:T(8,128)(2,1)S(1)} %get-tuple-element.53), channel_id=1, source_target_pairs={{0,4},{2,6},{4,0},{6,2},{1,5},{3,7},{5,1},{7,3},{8,12},{10,14},{12... | collective-permute-start | bytes 442376 | tf_op jit(solution)/shard_map/ppermute | solution.py:408
  93.6 20.6 %collective-permute-start.5 = (bf16[2,16,2304]{2,1,0:T(8,128)(2,1)S(1)}, bf16[2,16,2304]{2,1,0:T(8,128)(2,1)S(1)}, u32[]{:S(2)}, u32[]{:S(2)}) collective-permute-start(bf16[2,16,2304]{2,1,0:T(8,128)(2,1)S(1)} %get-tuple-element.54), channel_id=1, source_target_pairs={{0,6},{2,0},{4,2},{6,4},{1,7},{3,1},{5,3},{7,5},{8,14},{10,8},{12,... | collective-permute-start | bytes 442376 | tf_op jit(solution)/shard_map/ppermute | solution.py:408
  95.6 14.0 %collective-permute-start.21 = (bf16[2,4,16,2304]{3,2,1,0:T(8,128)(2,1)S(1)}, bf16[2,4,16,2304]{3,2,1,0:T(8,128)(2,1)S(1)}, u32[]{:S(2)}, u32[]{:S(2)}) collective-permute-start(bf16[2,4,16,2304]{3,2,1,0:T(8,128)(2,1)S(1)} %fusion), channel_id=1, source_target_pairs={{0,16},{8,24},{16,0},{24,8},{1,17},{9,25},{17,1},{25,9},{2,18},{10... | collective-permute-start | bytes 1769480 | tf_op jit(solution)/shard_map/ppermute | solution.py:405
  110.5 8.8 %collective-permute-start.22 = (bf16[2,16,2304]{2,1,0:T(8,128)(2,1)S(1)}, bf16[2,16,2304]{2,1,0:T(8,128)(2,1)S(1)}, u32[]{:S(2)}, u32[]{:S(2)}) collective-permute-start(bf16[2,16,2304]{2,1,0:T(8,128)(2,1)S(1)} %get-tuple-element.68), channel_id=1, source_target_pairs={{0,2},{2,4},{4,6},{6,0},{1,3},{3,5},{5,7},{7,1},{8,10},{10,12},{12... | collective-permute-start | bytes 442376 | tf_op jit(solution)/shard_map/ppermute | solution.py:408
  110.9 19.6 %collective-permute-start.23 = (bf16[2,16,2304]{2,1,0:T(8,128)(2,1)S(1)}, bf16[2,16,2304]{2,1,0:T(8,128)(2,1)S(1)}, u32[]{:S(2)}, u32[]{:S(2)}) collective-permute-start(bf16[2,16,2304]{2,1,0:T(8,128)(2,1)S(1)} %get-tuple-element.70), channel_id=1, source_target_pairs={{0,4},{2,6},{4,0},{6,2},{1,5},{3,7},{5,1},{7,3},{8,12},{10,14},{12... | collective-permute-start | bytes 442376 | tf_op jit(solution)/shard_map/ppermute | solution.py:408
  114.2 19.0 %collective-permute-start.24 = (bf16[2,16,2304]{2,1,0:T(8,128)(2,1)S(1)}, bf16[2,16,2304]{2,1,0:T(8,128)(2,1)S(1)}, u32[]{:S(2)}, u32[]{:S(2)}) collective-permute-start(bf16[2,16,2304]{2,1,0:T(8,128)(2,1)S(1)} %get-tuple-element.71), channel_id=1, source_target_pairs={{0,6},{2,0},{4,2},{6,4},{1,7},{3,1},{5,3},{7,5},{8,14},{10,8},{12,... | collective-permute-start | bytes 442376 | tf_op jit(solution)/shard_map/ppermute | solution.py:408
  114.3 19.8 %collective-permute-start.15 = (bf16[2,16,2304]{2,1,0:T(8,128)(2,1)S(1)}, bf16[2,16,2304]{2,1,0:T(8,128)(2,1)S(1)}, u32[]{:S(2)}, u32[]{:S(2)}) collective-permute-start(bf16[2,16,2304]{2,1,0:T(8,128)(2,1)S(1)} %fusion.9), channel_id=1, source_target_pairs={{0,2},{2,4},{4,6},{6,0},{1,3},{3,5},{5,7},{7,1},{8,10},{10,12},{12... | collective-permute-start | bytes 442376 | tf_op jit(solution)/shard_map/ppermute | solution.py:408
  116.4 21.3 %collective-permute-start.14 = (bf16[2,16,2304]{2,1,0:T(8,128)(2,1)S(1)}, bf16[2,16,2304]{2,1,0:T(8,128)(2,1)S(1)}, u32[]{:S(2)}, u32[]{:S(2)}) collective-permute-start(bf16[2,16,2304]{2,1,0:T(8,128)(2,1)S(1)} %fusion.9), channel_id=1, source_target_pairs={{0,4},{2,6},{4,0},{6,2},{1,5},{3,7},{5,1},{7,3},{8,12},{10,14},{12... | collective-permute-start | bytes 442376 | tf_op jit(solution)/shard_map/ppermute | solution.py:408
  119.3 24.9 %collective-permute-start.13 = (bf16[2,16,2304]{2,1,0:T(8,128)(2,1)S(1)}, bf16[2,16,2304]{2,1,0:T(8,128)(2,1)S(1)}, u32[]{:S(2)}, u32[]{:S(2)}) collective-permute-start(bf16[2,16,2304]{2,1,0:T(8,128)(2,1)S(1)} %fusion.9), channel_id=1, source_target_pairs={{0,6},{2,0},{4,2},{6,4},{1,7},{3,1},{5,3},{7,5},{8,14},{10,8},{12,... | collective-permute-start | bytes 442376 | tf_op jit(solution)/shard_map/ppermute | solution.py:408
  133.3 13.0 %collective-permute-start.27 = (bf16[2,16,2304]{2,1,0:T(8,128)(2,1)S(1)}, bf16[2,16,2304]{2,1,0:T(8,128)(2,1)S(1)}, u32[]{:S(2)}, u32[]{:S(2)}) collective-permute-start(bf16[2,16,2304]{2,1,0:T(8,128)(2,1)S(1)} %fusion.5), channel_id=1, source_target_pairs={{0,2},{2,4},{4,6},{6,0},{1,3},{3,5},{5,7},{7,1},{8,10},{10,12},{12... | collective-permute-start | bytes 442376 | tf_op jit(solution)/shard_map/ppermute | solution.py:408
  133.4 14.5 %collective-permute-start.26 = (bf16[2,16,2304]{2,1,0:T(8,128)(2,1)S(1)}, bf16[2,16,2304]{2,1,0:T(8,128)(2,1)S(1)}, u32[]{:S(2)}, u32[]{:S(2)}) collective-permute-start(bf16[2,16,2304]{2,1,0:T(8,128)(2,1)S(1)} %fusion.5), channel_id=1, source_target_pairs={{0,4},{2,6},{4,0},{6,2},{1,5},{3,7},{5,1},{7,3},{8,12},{10,14},{12... | collective-permute-start | bytes 442376 | tf_op jit(solution)/shard_map/ppermute | solution.py:408
  134.1 16.0 %collective-permute-start.25 = (bf16[2,16,2304]{2,1,0:T(8,128)(2,1)S(1)}, bf16[2,16,2304]{2,1,0:T(8,128)(2,1)S(1)}, u32[]{:S(2)}, u32[]{:S(2)}) collective-permute-start(bf16[2,16,2304]{2,1,0:T(8,128)(2,1)S(1)} %fusion.5), channel_id=1, source_target_pairs={{0,6},{2,0},{4,2},{6,4},{1,7},{3,1},{5,3},{7,5},{8,14},{10,8},{12,... | collective-permute-start | bytes 442376 | tf_op jit(solution)/shard_map/ppermute | solution.py:408
  144.3 16.3 %collective-permute-start.16 = (bf16[4,2,16,2304]{3,2,1,0:T(8,128)(2,1)S(1)}, bf16[4,2,16,2304]{3,2,1,0:T(8,128)(2,1)S(1)}, u32[]{:S(2)}, u32[]{:S(2)}) collective-permute-start(bf16[4,2,16,2304]{3,2,1,0:T(8,128)(2,1)S(1)} %pad_maximum_fusion.refs_0_), channel_id=1, source_target_pairs={{0,16},{8,24},{16,0},{24,8},{1,17},{9,25},{17,1},{25,9},{2,18},{10... | collective-permute-start | bytes 1769480 | tf_op jit(solution)/shard_map/ppermute | solution.py:405
  150.2 21.3 %collective-permute-start.28 = (bf16[4,2,16,2304]{3,2,1,0:T(8,128)(2,1)S(1)}, bf16[4,2,16,2304]{3,2,1,0:T(8,128)(2,1)S(1)}, u32[]{:S(2)}, u32[]{:S(2)}) collective-permute-start(bf16[4,2,16,2304]{3,2,1,0:T(8,128)(2,1)S(1)} %pad_maximum_fusion.1.refs_0_), channel_id=1, source_target_pairs={{0,16},{8,24},{16,0},{24,8},{1,17},{9,25},{17,1},{25,9},{2,18},{10... | collective-permute-start | bytes 1769480 | tf_op jit(solution)/shard_map/ppermute | solution.py:405
  150.8 20.7 %collective-permute-start.17 = (bf16[4,2,16,2304]{3,2,1,0:T(8,128)(2,1)S(1)}, bf16[4,2,16,2304]{3,2,1,0:T(8,128)(2,1)S(1)}, u32[]{:S(2)}, u32[]{:S(2)}) collective-permute-start(bf16[4,2,16,2304]{3,2,1,0:T(8,128)(2,1)S(1)} %pad_maximum_fusion.refs_0_), channel_id=1, source_target_pairs={{0,8},{8,0},{16,24},{24,16},{1,9},{9,1},{17,25},{25,17},{2,10},{10... | collective-permute-start | bytes 1769480 | tf_op jit(solution)/shard_map/ppermute | solution.py:405
  160.6 10.9 %collective-permute-start.18 = (bf16[4,2,16,2304]{3,2,1,0:T(8,128)(2,1)S(1)}, bf16[4,2,16,2304]{3,2,1,0:T(8,128)(2,1)S(1)}, u32[]{:S(2)}, u32[]{:S(2)}) collective-permute-start(bf16[4,2,16,2304]{3,2,1,0:T(8,128)(2,1)S(1)} %collective-permute-done.16.refs_1_), channel_id=1, source_target_pairs={{0,8},{8,0},{16,24},{24,16},{1,9},{9,1},{17,25},{25,17},{2,10},{10... | collective-permute-start | bytes 1769480 | tf_op jit(solution)/shard_map/ppermute | solution.py:405
  160.6 18.0 %collective-permute-start.29 = (bf16[4,2,16,2304]{3,2,1,0:T(8,128)(2,1)S(1)}, bf16[4,2,16,2304]{3,2,1,0:T(8,128)(2,1)S(1)}, u32[]{:S(2)}, u32[]{:S(2)}) collective-permute-start(bf16[4,2,16,2304]{3,2,1,0:T(8,128)(2,1)S(1)} %pad_maximum_fusion.1.refs_0_), channel_id=1, source_target_pairs={{0,8},{8,0},{16,24},{24,16},{1,9},{9,1},{17,25},{25,17},{2,10},{10... | collective-permute-start | bytes 1769480 | tf_op jit(solution)/shard_map/ppermute | solution.py:405
  171.5 7.2 %collective-permute-start.30 = (bf16[4,2,16,2304]{3,2,1,0:T(8,128)(2,1)S(1)}, bf16[4,2,16,2304]{3,2,1,0:T(8,128)(2,1)S(1)}, u32[]{:S(2)}, u32[]{:S(2)}) collective-permute-start(bf16[4,2,16,2304]{3,2,1,0:T(8,128)(2,1)S(1)} %collective-permute-done.28.refs_1_), channel_id=1, source_target_pairs={{0,8},{8,0},{16,24},{24,16},{1,9},{9,1},{17,25},{25,17},{2,10},{10... | collective-permute-start | bytes 1769480 | tf_op jit(solution)/shard_map/ppermute | solution.py:405
  178.1 26.1 %collective-permute-start.31 = (bf16[256,2048]{1,0:T(8,128)(2,1)S(1)}, bf16[256,2048]{1,0:T(8,128)(2,1)S(1)}, u32[]{:S(2)}, u32[]{:S(2)}) collective-permute-start(bf16[256,2048]{1,0:T(8,128)(2,1)S(1)} %get-tuple-element.73), channel_id=1, source_target_pairs={{0,1},{1,0},{2,3},{3,2},{4,5},{5,4},{6,7},{7,6},{8,9},{9,8},{10,11... | collective-permute-start | bytes 3145736 | tf_op jit(solution)/shard_map/ppermute | solution.py:402
  185.3 40.9 %collective-permute-start.32 = (bf16[256,2048]{1,0:T(8,128)(2,1)S(1)}, bf16[256,2048]{1,0:T(8,128)(2,1)S(1)}, u32[]{:S(2)}, u32[]{:S(2)}) collective-permute-start(bf16[256,2048]{1,0:T(8,128)(2,1)S(1)} %get-tuple-element.74), channel_id=1, source_target_pairs={{0,1},{1,0},{2,3},{3,2},{4,5},{5,4},{6,7},{7,6},{8,9},{9,8},{10,11... | collective-permute-start | bytes 3145736 | tf_op jit(solution)/shard_map/ppermute | solution.py:402
  186.9 39.3 %copy-start.2 = (bf16[512,2304]{1,0:T(8,128)(2,1)S(1)}, bf16[512,2304]{1,0:T(8,128)(2,1)}, u32[]{:S(2)}) copy-start(bf16[512,2304]{1,0:T(8,128)(2,1)} %get-tuple-element.42.rows_ref) | copy-start | bytes 7077892
